TPU v7x, 768 devices: a whole 4x8x12 slice. The times are simulated.
768 devices in a mesh: stream: 96 (over y, z), cross: 8 (over x, core).
Axes of the slice: x: 4, y: 8, z: 12, core: 2. Of those that a mesh axis runs over, the one named last changes fastest.
Arguments:
- fluid_state: float32 [5, 768, 64, 128], P(None, 'stream', 'cross'), may hold values from -6 to 6
- drop_xi: float32 [3, 96, 8, 8, 128], P(None, 'stream', 'cross'), may hold values from -1 to 1
- drop_vel: float32 [3, 96, 8, 8, 128], P(None, 'stream', 'cross'), may hold values from -4 to 4
- drop_tau: float32 [96, 8, 8, 128], P('stream', 'cross'), may hold values from 0.02 to 0.2
- drop_mass: float32 [96, 8, 8, 128], P('stream', 'cross'), may hold values from 0.5 to 5
- drop_host: int32 [96, 8, 8, 128], P('stream', 'cross'), may hold values from 0 to 15, as said below
- drop_alive: int32 [96, 8, 8, 128], P('stream', 'cross'), may hold values from 0 to 1, as said below
- depart_slots: int32 [96, 8, 256], P('stream', 'cross'), may hold values from 0 to 1023, as said below
- depart_count: int32 [96, 8], P('stream', 'cross'), may hold values from 0 to 256, as said below
- arrive_slots: int32 [96, 8, 256], P('stream', 'cross'), may hold values from 0 to 1023, as said below
- arrive_host: int32 [96, 8, 256], P('stream', 'cross'), may hold values from 0 to 15, as said below
- arrive_count: int32 [96, 8], P('stream', 'cross'), may hold values from 0 to 256, as said below
Outputs:
- new_state: float32 [5, 768, 64, 128], P(None, 'stream', 'cross')
- new_register: float32 [5, 768, 64, 128], P(None, 'stream', 'cross')
- drop_velocity: float32 [3, 96, 8, 8, 128], P(None, 'stream', 'cross')
- drop_register: float32 [3, 96, 8, 8, 128], P(None, 'stream', 'cross')
Inputs may be any that keep to these rules, and one draw needn't show every extreme that they name: `drop_host`: element of the slot's droplet among the 16 elements of its owner, numbered (a + e) * 16 + z by element coordinates; every departing droplet lies in the layer a = 0. `drop_alive`: every listed departure is live and every listed arrival slot is empty before it arrives. `depart_slots`: the first depart_count entries are distinct slots numbered block * 128 + slot, at most 32 of them in one block. `depart_count`: some device reaches 256. `arrive_slots`: the first arrive_count entries are distinct slots, entry i in the same block as entry i of the departure list of the previous slab's device with the same cross index. `arrive_host`: arriving droplets lie in the first element layer, the departing element's other coordinates kept. `arrive_count`: equals the departure count of the previous slab's device with the same cross index; zero on the first slab.
All inputs are finite; a program needn't handle non-finite values.
Results may differ from a plain program's by a relative error of at most 0.0003.
Values sent between devices are 32-bit elements; how exact they have to be, the bound alone decides.
No kernel may reach another device: no remote copies, remote signals or barrier semaphores. Data moves between devices by JAX's collectives and lax.ppermute only.
A program may use at most 64 MiB of HBM per device.

v0:
```python
import jax
import jax.numpy as jnp
import numpy as np
from jax import lax
from jax.experimental import pallas as pl
from jax.experimental.pallas import tpu as pltpu
from jax.sharding import PartitionSpec as P

LIFT = 28.0
STEP_SIZE = 0.02
COEF_A = (0.0, -567301805773.0 / 1357537059087.0)
COEF_B = (1432997174477.0 / 9575080441755.0, 5161836677717.0 / 13612068292357.0)
F32 = jnp.float32
BF16 = jnp.bfloat16

TAU, LOAD, HOST, OUT_POS, IN_POS, IN_HOST, ALIVE = 6, 7, 8, 9, 10, 11, 12
PLANES = 16


def lgl_tables():
    node_pos = np.array(
        [
            -1.0,
            -0.871740148509607,
            -0.591700181433142,
            -0.209299217902479,
            0.209299217902479,
            0.591700181433142,
            0.871740148509607,
            1.0,
        ]
    )
    bary_wts = np.array(
        [1.0 / np.prod([node_pos[a] - node_pos[b] for b in range(8) if b != a]) for a in range(8)]
    )
    deriv_mat = np.zeros((8, 8))
    for a in range(8):
        for b in range(8):
            if a != b:
                deriv_mat[a, b] = bary_wts[b] / bary_wts[a] / (node_pos[a] - node_pos[b])
        deriv_mat[a, a] = -np.sum(deriv_mat[a])
    return (node_pos, bary_wts, deriv_mat)


NODES, BARY, DERIV = lgl_tables()


def column_planes():
    rows = [BARY]
    rows += [np.roll(NODES, -t) for t in range(1, 8)]
    rows += [-DERIV[:, j] for j in range(8)]
    rows += [0.5 * (1.0 + NODES)]
    rows += [LIFT * (np.arange(8) == 0), LIFT * (np.arange(8) == 7)]
    table = np.stack(rows).astype(np.float32)
    return np.ascontiguousarray(np.broadcast_to(table[:, :, None], table.shape + (128,)))


def span_matrix():
    full = np.zeros((128, 128))
    for e in range(16):
        base = 8 * e
        full[base : base + 8, base : base + 8] -= DERIV.T
        full[(base - 1) % 128, base] += 0.5 * LIFT
        full[base, base] -= 0.5 * LIFT
        full[(base + 8) % 128, base + 7] -= 0.5 * LIFT
        full[base + 7, base + 7] += 0.5 * LIFT
    high = full.astype(np.float32).astype(jnp.bfloat16)
    low = (full - high.astype(np.float64)).astype(np.float32).astype(jnp.bfloat16)
    return np.concatenate([high, high, low], axis=0)


def two_parts(values):
    high = values.astype(BF16)
    return high, (values - high.astype(F32)).astype(BF16)


def three_parts(values):
    high = values.astype(BF16)
    rest = values - high.astype(F32)
    mid = rest.astype(BF16)
    low = (rest - mid.astype(F32)).astype(BF16)
    return jnp.concatenate([high, mid, low], axis=0)


def dot_rows(left, right):
    return lax.dot_general(left, right, (((1,), (1,)), ((), ())), preferred_element_type=F32)


def dot_plain(left, right):
    return lax.dot_general(left, right, (((1,), (0,)), ((), ())), preferred_element_type=F32)


def row(values, index):
    return jnp.broadcast_to(values[index : index + 1], (8, values.shape[1]))


def flag(mask):
    return jnp.where(mask, 1.0, 0.0)


def mean_profile(cols):
    width = float(lax.axis_size("cross"))
    coord_y = lax.axis_index("cross").astype(F32) + cols[16]
    return 0.1 + 0.4 * (1.0 + jnp.tanh(2.0 * (0.25 * width - jnp.abs(coord_y - 0.5 * width))))


def basis(coord_row, cols):
    coord = jnp.broadcast_to(coord_row, (8, 128))
    value = cols[0] * (coord - cols[1])
    for t in range(2, 8):
        value = value * (coord - cols[t])
    return value


def list_planes(dep, dep_count, arr, arr_host, arr_count):
    lanes = dep.shape[1]
    lane = lax.broadcasted_iota(jnp.int32, (1, lanes), 1)
    block_no = lax.broadcasted_iota(jnp.int32, (8, lanes), 0)
    slot_no = lax.broadcasted_iota(jnp.int32, (128, lanes), 0)

    def member(slots, count):
        block = jnp.where(lane < count, slots >> 7, -1)
        return flag(block_no == block)

    dep_in, arr_in = member(dep, dep_count), member(arr, arr_count)
    earlier = flag(
        lax.broadcasted_iota(jnp.int32, (lanes, lanes), 0)
        < lax.broadcasted_iota(jnp.int32, (lanes, lanes), 1)
    ).astype(BF16)
    both = jnp.concatenate([dep_in, arr_in], axis=0)
    ranks = both * (dot_plain(both.astype(BF16), earlier) + 1.0)
    dep_hot = flag(slot_no == (dep & 127)).astype(BF16)
    arr_hot = flag(slot_no == (arr & 127)).astype(BF16)
    out_pos = dot_rows(ranks[:8].astype(BF16), dep_hot)
    arr_rows = jnp.concatenate([ranks[8:], arr_in * arr_host.astype(F32)], axis=0)
    landed = dot_rows(arr_rows.astype(BF16), arr_hot)
    return out_pos, landed[:8], landed[8:]


def send_kernel(
    state, xi, vel, tau, mass, host, alive, dep, dep_count, arr, arr_host, arr_count,
    out, x_first, x_last, y_first, y_last,
):
    x_first[...] = state[:, 0]
    x_last[...] = state[:, 7]
    y_first[...] = state[:, :, 0, :]
    y_last[...] = state[:, :, 7, :]
    live = alive[...].astype(F32)
    out_pos, in_pos, in_host = list_planes(
        dep[...], dep_count[0, 0], arr[...], arr_host[...], arr_count[0, 0]
    )
    for a in range(3):
        out[:, a, :] = xi[a]
        out[:, 3 + a, :] = vel[a]
    out[:, TAU, :] = tau[...]
    out[:, LOAD, :] = mass[...] * live
    out[:, HOST, :] = host[...].astype(F32)
    out[:, OUT_POS, :] = out_pos
    out[:, IN_POS, :] = in_pos
    out[:, IN_HOST, :] = in_host
    out[:, ALIVE, :] = live
    for r in range(ALIVE + 1, PLANES):
        out[:, r, :] = jnp.zeros((8, 128), F32)


def fill_weights(c, coords, host_row, cols, w, l1, l2):
    lanes = pl.ds(128 * c, 128)
    l1[:, lanes] = basis(coords[0:1], cols)
    l2[:, lanes] = basis(coords[1:2], cols)
    third = basis(coords[2:3], cols)
    high = third.astype(BF16).astype(F32)
    low = third - high
    host = jnp.broadcast_to(host_row, (8, 128))
    zero = jnp.zeros((8, 128), F32)
    for e in range(0, 16, 2):
        here, after = host == float(e), host == float(e + 1)
        rows_h = jnp.concatenate(
            [jnp.where(here, high, zero), jnp.where(after, high, zero)], axis=0
        ).astype(BF16)
        rows_l = jnp.concatenate(
            [jnp.where(here, low, zero), jnp.where(after, low, zero)], axis=0
        ).astype(BF16)
        w[pl.ds(8 * e, 16), lanes] = rows_h
        w[pl.ds(128 + 8 * e, 16), lanes] = rows_h
        w[pl.ds(256 + 8 * e, 16), lanes] = rows_l


def sample_all(state, mean_flow, w, s):
    fields = jnp.concatenate([state[1] + mean_flow[None], state[2], state[3]], axis=0)
    high, low = two_parts(fields.reshape(192, 128))
    s[...] = dot_plain(jnp.concatenate([high, low, high], axis=1), w[...])


def fluid_rows(c, s, l1, l2):
    lanes = pl.ds(128 * c, 128)
    along_x, along_y = l1[:, lanes], l2[:, lanes]
    rows = []
    for a in range(3):
        total = None
        for i in range(8):
            term = row(along_x, i) * s[pl.ds(64 * a + 8 * i, 8), lanes]
            total = term if total is None else total + term
        rows.append(jnp.sum(total * along_y, axis=0, keepdims=True))
    return jnp.concatenate(rows, axis=0)


def fill_force(c, force, l1, l2, fh, fl):
    lanes = pl.ds(128 * c, 128)
    along_x, along_y = l1[:, lanes], l2[:, lanes]
    pushes = [-row(force, a) for a in range(3)]
    for i in range(0, 8, 2):
        plane = jnp.concatenate([row(along_x, i) * along_y, row(along_x, i + 1) * along_y], axis=0)
        for a in range(3):
            high, low = two_parts(plane * jnp.concatenate([pushes[a], pushes[a]], axis=0))
            fh[pl.ds(64 * a + 8 * i, 16), lanes] = high
            fl[pl.ds(64 * a + 8 * i, 16), lanes] = low


def deposit_all(w, fh, fl):
    high, low = w[0:128, :], w[256:384, :]
    total = dot_rows(fh[...], high) + dot_rows(fl[...], high) + dot_rows(fh[...], low)
    return total.reshape(3, 8, 8, 128)


def flux_x(q, mean_flow):
    return [
        mean_flow * q[0] + q[1],
        mean_flow * q[1] + q[4],
        mean_flow * q[2],
        mean_flow * q[3],
        mean_flow * q[4] + q[1],
    ]


def fluid_rate(state, low_x, high_x, low_y, high_y, mean_flow, cols, mz):
    q = [[state[v, i] for i in range(8)] for v in range(5)]
    both = jnp.concatenate([state[3].reshape(64, 128), state[4].reshape(64, 128)], axis=0)
    high, low = two_parts(both)
    spans = dot_plain(jnp.concatenate([high, low, high], axis=1), mz[...])
    spans = spans.reshape(2, 8, 8, 128)
    node = lax.broadcasted_iota(jnp.int32, (8, 128), 1) & 7
    first, edge = node == 0, LIFT * flag((node == 0) | (node == 7))
    flow = [flux_x([q[v][i] for v in range(5)], mean_flow) for i in range(8)]
    lows = [low_x[v] for v in range(5)]
    highs = [high_x[v] for v in range(5)]
    flow_low, flow_high = flux_x(lows, mean_flow), flux_x(highs, mean_flow)
    first_y, last_y = cols[17], cols[18]
    half_first, half_last = 0.5 * first_y, 0.5 * last_y
    result = [[None] * 8 for _ in range(5)]
    for i in range(8):
        below = [row(low_y[v], i) for v in range(5)]
        above = [row(high_y[v], i) for v in range(5)]
        slopes = {}
        for v in (2, 4):
            value = q[v][i]
            slope = half_first * (below[v] - value) - half_last * (above[v] - value)
            for j in range(8):
                slope = slope + cols[8 + j] * row(value, j)
            slopes[v] = slope
        for v in range(5):
            value = q[v][i]
            total = -float(DERIV[i, 0]) * flow[0][v]
            for b in range(1, 8):
                if DERIV[i, b] != 0.0:
                    total = total - float(DERIV[i, b]) * flow[b][v]
            if i == 0:
                total = total + (0.5 * LIFT) * (flow_low[v] - flow[0][v])
                total = total - LIFT * (value - lows[v])
            if i == 7:
                total = total - (0.5 * LIFT) * (flow_high[v] - flow[7][v])
                total = total + LIFT * (highs[v] - value)
            total = total + first_y * (below[v] - value) + last_y * (above[v] - value)
            if v in (0, 4):
                total = total + slopes[2]
            if v == 2:
                total = total + slopes[4]
            beside = jnp.where(first, pltpu.roll(value, 1, 1), pltpu.roll(value, 127, 1))
            total = total + edge * (beside - value)
            if v in (0, 4):
                total = total + spans[0, i]
            if v == 3:
                total = total + spans[1, i]
            result[v][i] = total
    return result


def droplets_first(planes, cols, w, l1, l2):
    for c in range(8):
        block = planes[c]
        fill_weights(c, block[0:3], block[HOST : HOST + 1], cols, w, l1, l2)


def first_kernel(
    state, low_x, high_x, low_y, high_y, planes, cols_ref, mz,
    state_out, reg_out, forward, x_first, y_first, y_last, drop_out,
    w, s, l1, l2, fh, fl,
):
    cols = [cols_ref[t] for t in range(cols_ref.shape[0])]
    mean_flow = mean_profile(cols)
    droplets_first(planes, cols, w, l1, l2)
    sample_all(state, mean_flow, w, s)
    seat = lax.broadcasted_iota(jnp.int32, (128, 128), 0).astype(F32)
    records, seats = [], []
    for c in range(8):
        block = planes[c]
        fluid = fluid_rows(c, s, l1, l2)
        accel = (fluid - block[3:6]) / block[TAU : TAU + 1]
        register = STEP_SIZE * accel
        velocity = block[3:6] + COEF_B[0] * register
        drop_out[c] = jnp.concatenate([velocity, register, jnp.zeros((2, 128), F32)], axis=0)
        fill_force(c, accel * block[LOAD : LOAD + 1], l1, l2, fh, fl)
        records.append(
            jnp.concatenate(
                [block[0:3], velocity, block[TAU : LOAD + 1], register, jnp.zeros((5, 128), F32)],
                axis=0,
            )
        )
        out_pos = block[OUT_POS : OUT_POS + 1]
        place = jnp.where(out_pos > 0.5, out_pos + float(32 * (c % 4) - 1), -1.0)
        seats.append(flag(seat == place).astype(BF16))
    for g in range(2):
        group = slice(4 * g, 4 * g + 4)
        packed = dot_rows(
            three_parts(jnp.concatenate(records[group], axis=1)),
            jnp.concatenate(seats[group], axis=1),
        )
        packed = packed[0:16] + packed[16:32] + packed[32:48]
        forward[5 + 2 * g] = packed[0:8]
        forward[6 + 2 * g] = packed[8:16]
    source = deposit_all(w, fh, fl)
    rate = fluid_rate(state, low_x, high_x, low_y, high_y, mean_flow, cols, mz)
    for v in range(5):
        for i in range(8):
            total = rate[v][i] + source[v - 1, i] if 1 <= v <= 3 else rate[v][i]
            register = STEP_SIZE * total
            value = state[v, i] + COEF_B[0] * register
            reg_out[v, i] = register
            state_out[v, i] = value
            y_first[v, pl.ds(i, 1), :] = value[0:1]
            y_last[v, pl.ds(i, 1), :] = value[7:8]
            if i == 0:
                x_first[v] = value
            if i == 7:
                forward[v] = value


def second_kernel(
    state, reg_in, low_x, high_x, low_y, high_y, planes, drops, cols_ref, mz,
    state_out, reg_out, back,
    w, s, l1, l2, fh, fl, held,
):
    cols = [cols_ref[t] for t in range(cols_ref.shape[0])]
    mean_flow = mean_profile(cols)
    seat = lax.broadcasted_iota(jnp.int32, (128, 128), 0).astype(F32)
    arrived = []
    for g in range(2):
        packed = jnp.concatenate([low_x[5 + 2 * g], low_x[6 + 2 * g]], axis=0)
        seats = []
        for c in range(4 * g, 4 * g + 4):
            in_pos = planes[c, IN_POS : IN_POS + 1]
            place = jnp.where(in_pos > 0.5, in_pos + float(32 * (c % 4) - 1), -1.0)
            seats.append(flag(seat == place).astype(BF16))
        landed = dot_plain(three_parts(packed), jnp.concatenate(seats, axis=1))
        arrived.append(landed[0:16] + landed[16:32] + landed[32:48])
    for c in range(8):
        block, drop = planes[c], drops[c]
        landed = arrived[c // 4][:, 128 * (c % 4) : 128 * (c % 4) + 128]
        stays = flag(block[OUT_POS : OUT_POS + 1] < 0.5)
        fresh = block[IN_POS : IN_POS + 1] > 0.5
        load = jnp.where(fresh, landed[LOAD : LOAD + 1], block[LOAD : LOAD + 1] * stays)
        live = jnp.where(fresh, 1.0, block[ALIVE : ALIVE + 1] * stays)
        host = jnp.where(fresh, block[IN_HOST : IN_HOST + 1], block[HOST : HOST + 1])
        tau = jnp.where(fresh, landed[TAU : TAU + 1], block[TAU : TAU + 1])
        fresh3 = jnp.broadcast_to(block[IN_POS : IN_POS + 1], (3, 128)) > 0.5
        coords = jnp.where(fresh3, landed[0:3], block[0:3])
        velocity = jnp.where(fresh3, landed[3:6], drop[0:3])
        register = jnp.where(fresh3, landed[8:11], drop[3:6])
        held[c] = jnp.concatenate(
            [velocity, register, tau, load, live, jnp.zeros((7, 128), F32)], axis=0
        )
        fill_weights(c, coords, host, cols, w, l1, l2)
    sample_all(state, mean_flow, w, s)
    for c in range(8):
        block = held[c]
        fluid = fluid_rows(c, s, l1, l2)
        accel = (fluid - block[0:3]) / block[6:7]
        fill_force(c, accel * block[7:8], l1, l2, fh, fl)
        register = COEF_A[1] * block[3:6] + STEP_SIZE * accel
        velocity = block[0:3] + COEF_B[1] * register
        live = block[8:9]
        back[c] = jnp.concatenate(
            [velocity * live, register * live, jnp.zeros((2, 128), F32)], axis=0
        )
    source = deposit_all(w, fh, fl)
    rate = fluid_rate(state, low_x, high_x, low_y, high_y, mean_flow, cols, mz)
    for v in range(5):
        for i in range(8):
            total = rate[v][i] + source[v - 1, i] if 1 <= v <= 3 else rate[v][i]
            register = COEF_A[1] * reg_in[v, i] + STEP_SIZE * total
            reg_out[v, i] = register
            state_out[v, i] = state[v, i] + COEF_B[1] * register


def last_kernel(returned, vel_out, reg_out):
    for a in range(3):
        vel_out[a] = returned[:, a, :]
        reg_out[a] = returned[:, 3 + a, :]


def moved(block, axis, step):
    count = lax.axis_size(axis)
    route = [(i, i + step) for i in range(count) if 0 <= i + step < count]
    return lax.ppermute(block, axis, route)


def shape(*dims):
    return jax.ShapeDtypeStruct(dims, F32)


VMEM = pl.BlockSpec(memory_space=pltpu.VMEM)
SMEM = pl.BlockSpec(memory_space=pltpu.SMEM)
ROOM = pltpu.CompilerParams(vmem_limit_bytes=12 * 1024 * 1024)
WORK = [
    pltpu.VMEM((384, 1024), BF16),
    pltpu.VMEM((192, 1024), F32),
    pltpu.VMEM((8, 1024), F32),
    pltpu.VMEM((8, 1024), F32),
    pltpu.VMEM((192, 1024), BF16),
    pltpu.VMEM((192, 1024), BF16),
]


def local(
    fluid_state,
    drop_xi,
    drop_vel,
    drop_tau,
    drop_mass,
    drop_host,
    drop_alive,
    depart_slots,
    depart_count,
    arrive_slots,
    arrive_host,
    arrive_count,
):
    lanes = depart_slots.shape[-1]
    cols = jnp.asarray(column_planes())
    mz = jnp.asarray(span_matrix())
    face = shape(5, 8, 128)
    payload, x_first, x_last, y_first, y_last = pl.pallas_call(
        send_kernel,
        out_shape=(shape(8, PLANES, 128), face, face, face, face),
        in_specs=[VMEM] * 8 + [SMEM, VMEM, VMEM, SMEM],
        out_specs=(VMEM,) * 5,
        compiler_params=ROOM,
        name="send",
    )(
        fluid_state,
        drop_xi.reshape(3, 8, 128),
        drop_vel.reshape(3, 8, 128),
        drop_tau.reshape(8, 128),
        drop_mass.reshape(8, 128),
        drop_host.reshape(8, 128),
        drop_alive.reshape(8, 128),
        depart_slots.reshape(1, lanes),
        depart_count.reshape(1, 1),
        arrive_slots.reshape(1, lanes),
        arrive_host.reshape(1, lanes),
        arrive_count.reshape(1, 1),
    )
    planes = lax.all_to_all(payload, "cross", split_axis=0, concat_axis=0, tiled=True)
    low_x, high_x = moved(x_last, "stream", 1), moved(x_first, "stream", -1)
    low_y, high_y = moved(y_last, "cross", 1), moved(y_first, "cross", -1)
    state, register, forward, x_first, y_first, y_last, drops = pl.pallas_call(
        first_kernel,
        out_shape=(
            shape(5, 8, 8, 128),
            shape(5, 8, 8, 128),
            shape(9, 8, 128),
            face,
            face,
            face,
            shape(8, 8, 128),
        ),
        in_specs=[VMEM] * 8,
        out_specs=(VMEM,) * 7,
        scratch_shapes=WORK,
        compiler_params=ROOM,
        name="section_1",
    )(fluid_state, low_x, high_x, low_y, high_y, planes, cols, mz)
    low_x, high_x = moved(forward, "stream", 1), moved(x_first, "stream", -1)
    low_y, high_y = moved(y_last, "cross", 1), moved(y_first, "cross", -1)
    state, register, back = pl.pallas_call(
        second_kernel,
        out_shape=(shape(5, 8, 8, 128), shape(5, 8, 8, 128), shape(8, 8, 128)),
        in_specs=[VMEM] * 10,
        out_specs=(VMEM,) * 3,
        scratch_shapes=WORK + [pltpu.VMEM((8, 16, 128), F32)],
        compiler_params=ROOM,
        name="section_2",
    )(state, register, low_x, high_x, low_y, high_y, planes, drops, cols, mz)
    returned = lax.all_to_all(back, "cross", split_axis=0, concat_axis=0, tiled=True)
    velocity, drop_reg = pl.pallas_call(
        last_kernel,
        out_shape=(shape(3, 8, 128), shape(3, 8, 128)),
        in_specs=[VMEM],
        out_specs=(VMEM, VMEM),
        compiler_params=ROOM,
        name="give",
    )(returned)
    return (state, register, velocity.reshape(drop_vel.shape), drop_reg.reshape(drop_vel.shape))


def solution(mesh):
    placed = (
        P(None, "stream", "cross", None),
        P(None, "stream", "cross", None, None),
        P(None, "stream", "cross", None, None),
        P("stream", "cross", None, None),
        P("stream", "cross", None, None),
        P("stream", "cross", None, None),
        P("stream", "cross", None, None),
        P("stream", "cross", None),
        P("stream", "cross"),
        P("stream", "cross", None),
        P("stream", "cross", None),
        P("stream", "cross"),
    )
    return jax.shard_map(
        local,
        mesh=mesh,
        in_specs=placed,
        out_specs=(
            P(None, "stream", "cross", None),
            P(None, "stream", "cross", None),
            P(None, "stream", "cross", None, None),
            P(None, "stream", "cross", None, None),
        ),
        check_vma=False,
    )
```

profile of v0, /device:TPU:32, one launch (start us, length us, event | category | flops | bytes accessed | tf_op | source)
XLA Modules:
  0.0 67.8 jit_solution(1104303765247248933)
XLA Ops:
  0.6 0.0 copy-start.4
  1.9 0.0 copy-start.7
  2.0 0.0 copy-start.6
  2.0 0.0 copy-done.4
  2.0 0.7 copy-done.7
  2.6 0.0 copy-done.6
  2.7 0.0 copy-start
  2.7 0.9 %copy-done = f32[5,8,8,128]{3,2,1,0:T(8,128)S(1)} copy-done((f32[5,8,8,128]{3,2,1,0:T(8,128)S(1)}, f32[5,8,8,128]{3,2,1,0:T(8,128)}, u32[]{:S(2)}) %copy-start) | copy-done | bytes 163864
  3.6 0.0 copy-start.5
  3.6 0.7 %copy-done.5 = f32[3,1,1,8,128]{4,3,2,1,0:T(8,128)S(1)} copy-done((f32[3,1,1,8,128]{4,3,2,1,0:T(8,128)S(1)}, f32[3,1,1,8,128]{4,3,2,1,0:T(8,128)}, u32[]{:S(2)}) %copy-start.5) | copy-done | bytes 12312
  4.3 0.0 copy-start.8
  4.3 0.7 %copy-done.8 = s32[1,1,8,128]{3,2,1,0:T(8,128)S(1)} copy-done((s32[1,1,8,128]{3,2,1,0:T(8,128)S(1)}, s32[1,1,8,128]{3,2,1,0:T(8,128)}, u32[]{:S(2)}) %copy-start.8) | copy-done | bytes 4120
  5.0 0.0 copy-start.9
  5.0 0.7 %copy-done.9 = s32[1,1,8,128]{3,2,1,0:T(8,128)S(1)} copy-done((s32[1,1,8,128]{3,2,1,0:T(8,128)S(1)}, s32[1,1,8,128]{3,2,1,0:T(8,128)}, u32[]{:S(2)}) %copy-start.9) | copy-done | bytes 4120
  5.7 0.0 copy-start.10
  5.7 0.7 copy-done.10
  6.3 0.0 copy-start.11
  6.3 0.7 copy-done.11
  7.0 0.0 copy-start.12
  7.0 0.7 copy-done.12
  7.7 0.0 copy-start.1
  7.7 0.0 copy-start.3
  7.7 0.9 %send.1 = (f32[8,16,128]{2,1,0:T(8,128)}, f32[5,8,128]{2,1,0:T(8,128)S(1)}, f32[5,8,128]{2,1,0:T(8,128)S(1)}, f32[5,8,128]{2,1,0:T(8,128)S(1)}, f32[5,8,128]{2,1,0:T(8,128)S(1)}) custom-call(f32[5,8,8,128]{3,2,1,0:T(8,128)S(1)} %copy-done, f32[3,8,128]{2,1,0:T(8,128)S(1)} %bitcast.15, f32[3,8,128]{2,1,0:T(8,128)S(1)} %bitcast.16, f32[8,128]{1,0:T(8,128)S(1)} %bitcast.17, ...), custom_call_target="tpu_custom_call" | custom-call | tf_op jit(solution)/shard_map/send/pallas_call | solution.py:451
  8.6 4.4 %all-to-all-start = ((f32[8,16,128]{2,1,0:T(8,128)}), f32[8,16,128]{2,1,0:T(8,128)S(1)}, u32[]{:S(2)}, u32[]{:S(2)}) async-start(f32[8,16,128]{2,1,0:T(8,128)} %get-tuple-element.25), calls=%async_computation | async-start | bytes 131072 | tf_op jit(solution)/shard_map/all_to_all | solution.py:472
  13.1 4.3 %collective-permute-start = (f32[5,8,128]{2,1,0:T(8,128)S(1)}, f32[5,8,128]{2,1,0:T(8,128)S(1)}, u32[]{:S(2)}, u32[]{:S(2)}) collective-permute-start(f32[5,8,128]{2,1,0:T(8,128)S(1)} %get-tuple-element.21), channel_id=1, source_target_pairs={{0,8},{8,16},{16,24},{24,32},{32,40},{40,48},{48,56},{56,64},{64,7... | collective-permute-start | bytes 61448 | tf_op jit(solution)/shard_map/ppermute | solution.py:413
  17.3 12.1 %collective-permute-start.1 = (f32[5,8,128]{2,1,0:T(8,128)S(1)}, f32[5,8,128]{2,1,0:T(8,128)S(1)}, u32[]{:S(2)}, u32[]{:S(2)}) collective-permute-start(f32[5,8,128]{2,1,0:T(8,128)S(1)} %get-tuple-element.22), channel_id=1, source_target_pairs={{8,0},{16,8},{24,16},{32,24},{40,32},{48,40},{56,48},{64,56},{72,6... | collective-permute-start | bytes 61448 | tf_op jit(solution)/shard_map/ppermute | solution.py:413
  29.5 2.1 %collective-permute-start.2 = (f32[5,8,128]{2,1,0:T(8,128)S(1)}, f32[5,8,128]{2,1,0:T(8,128)S(1)}, u32[]{:S(2)}, u32[]{:S(2)}) collective-permute-start(f32[5,8,128]{2,1,0:T(8,128)S(1)} %get-tuple-element.23), channel_id=1, source_target_pairs={{0,1},{1,2},{2,3},{3,4},{4,5},{5,6},{6,7},{8,9},{9,10},{10,11},{11... | collective-permute-start | bytes 61448 | tf_op jit(solution)/shard_map/ppermute | solution.py:413
  31.6 1.3 %collective-permute-start.3 = (f32[5,8,128]{2,1,0:T(8,128)S(1)}, f32[5,8,128]{2,1,0:T(8,128)S(1)}, u32[]{:S(2)}, u32[]{:S(2)}) collective-permute-start(f32[5,8,128]{2,1,0:T(8,128)S(1)} %get-tuple-element.24), channel_id=1, source_target_pairs={{1,0},{2,1},{3,2},{4,3},{5,4},{6,5},{7,6},{9,8},{10,9},{11,10},{12... | collective-permute-start | bytes 61448 | tf_op jit(solution)/shard_map/ppermute | solution.py:413
  32.9 0.0 collective-permute-done.low_x
  32.9 0.0 collective-permute-done.1.high_x
  32.9 0.0 collective-permute-done.2.low_y
  32.9 3.2 %collective-permute-done.3.high_y = f32[5,8,128]{2,1,0:T(8,128)S(1)} collective-permute-done((f32[5,8,128]{2,1,0:T(8,128)S(1)}, f32[5,8,128]{2,1,0:T(8,128)S(1)}, u32[]{:S(2)}, u32[]{:S(2)}) %collective-permute-start.3) | collective-permute-done | bytes 20512 | tf_op jit(solution)/shard_map/ppermute | solution.py:413
  36.1 0.0 all-to-all-done.planes
  36.1 0.0 copy-done.1
  36.1 0.0 copy-done.3
  36.1 0.0 copy-done.2
  36.1 1.3 %section_1.1 = (f32[5,8,8,128]{3,2,1,0:T(8,128)S(1)}, f32[5,8,8,128]{3,2,1,0:T(8,128)S(1)}, f32[9,8,128]{2,1,0:T(8,128)S(1)}, f32[5,8,128]{2,1,0:T(8,128)S(1)}, ...) custom-call(f32[5,8,8,128]{3,2,1,0:T(8,128)S(1)} %copy-done.1, ...), custom_call_target="tpu_custom_call" | custom-call | tf_op jit(solution)/shard_map/section_1/pallas_call | solution.py:475
  37.4 1.9 %collective-permute-start.4 = (f32[9,8,128]{2,1,0:T(8,128)S(1)}, f32[9,8,128]{2,1,0:T(8,128)S(1)}, u32[]{:S(2)}, u32[]{:S(2)}) collective-permute-start(f32[9,8,128]{2,1,0:T(8,128)S(1)} %get-tuple-element.28), channel_id=1, source_target_pairs={{0,8},{8,16},{16,24},{24,32},{32,40},{40,48},{48,56},{56,64},{64,7... | collective-permute-start | bytes 110600 | tf_op jit(solution)/shard_map/ppermute | solution.py:413
  39.3 7.2 %collective-permute-start.5 = (f32[5,8,128]{2,1,0:T(8,128)S(1)}, f32[5,8,128]{2,1,0:T(8,128)S(1)}, u32[]{:S(2)}, u32[]{:S(2)}) collective-permute-start(f32[5,8,128]{2,1,0:T(8,128)S(1)} %get-tuple-element.29), channel_id=1, source_target_pairs={{8,0},{16,8},{24,16},{32,24},{40,32},{48,40},{56,48},{64,56},{72,6... | collective-permute-start | bytes 61448 | tf_op jit(solution)/shard_map/ppermute | solution.py:413
  46.6 3.9 %collective-permute-start.6 = (f32[5,8,128]{2,1,0:T(8,128)S(1)}, f32[5,8,128]{2,1,0:T(8,128)S(1)}, u32[]{:S(2)}, u32[]{:S(2)}) collective-permute-start(f32[5,8,128]{2,1,0:T(8,128)S(1)} %get-tuple-element.30), channel_id=1, source_target_pairs={{0,1},{1,2},{2,3},{3,4},{4,5},{5,6},{6,7},{8,9},{9,10},{10,11},{11... | collective-permute-start | bytes 61448 | tf_op jit(solution)/shard_map/ppermute | solution.py:413
  50.5 1.3 %collective-permute-start.7 = (f32[5,8,128]{2,1,0:T(8,128)S(1)}, f32[5,8,128]{2,1,0:T(8,128)S(1)}, u32[]{:S(2)}, u32[]{:S(2)}) collective-permute-start(f32[5,8,128]{2,1,0:T(8,128)S(1)} %get-tuple-element.31), channel_id=1, source_target_pairs={{1,0},{2,1},{3,2},{4,3},{5,4},{6,5},{7,6},{9,8},{10,9},{11,10},{12... | collective-permute-start | bytes 61448 | tf_op jit(solution)/shard_map/ppermute | solution.py:413
  51.8 0.0 collective-permute-done.5.high_x
  51.8 0.0 collective-permute-done.6.low_y
  51.8 1.8 %collective-permute-done.7.high_y = f32[5,8,128]{2,1,0:T(8,128)S(1)} collective-permute-done((f32[5,8,128]{2,1,0:T(8,128)S(1)}, f32[5,8,128]{2,1,0:T(8,128)S(1)}, u32[]{:S(2)}, u32[]{:S(2)}) %collective-permute-start.7) | collective-permute-done | bytes 20512 | tf_op jit(solution)/shard_map/ppermute | solution.py:413
  53.6 0.0 collective-permute-done.4.low_x
  53.6 2.2 %section_2.1 = (f32[5,8,8,128]{3,2,1,0:T(8,128)}, f32[5,8,8,128]{3,2,1,0:T(8,128)}, f32[8,8,128]{2,1,0:T(8,128)S(1)}) custom-call(f32[5,8,8,128]{3,2,1,0:T(8,128)S(1)} %get-tuple-element.26.state, f32[5,8,8,128]{3,2,1,0:T(8,128)S(1)} %get-tuple-element.27.reg_in, f32[9,8,128]{2,1,0:T(8,128)S(1)} %collective-permute-done.4.low_x, ...), custom_call_target="tpu_custom_call" | custom-call | tf_op jit(solution)/shard_map/section_2/pallas_call | solution.py:494
  55.8 11.3 %all_to_all.10.returned = f32[8,8,128]{2,1,0:T(8,128)S(1)} all-to-all(f32[8,8,128]{2,1,0:T(8,128)S(1)} %get-tuple-element.35), channel_id=1, replica_groups=mesh['stream'=96,'cross'=8] {'cross'}, dimensions={0} | all-to-all | bytes 65536 | tf_op jit(solution)/shard_map/all_to_all | solution.py:503
  67.2 0.6 give.1
  (1 shorter events, 0.0 us)
Async XLA Ops:
  0.6 1.3 %copy-start.4 = (f32[3,1,1,8,128]{4,3,2,1,0:T(8,128)S(1)}, f32[3,1,1,8,128]{4,3,2,1,0:T(8,128)}, u32[]{:S(2)}) copy-start(f32[3,1,1,8,128]{4,3,2,1,0:T(8,128)} %param.15) | copy-start | bytes 36868
  1.9 0.7 %copy-start.7 = (f32[1,1,8,128]{3,2,1,0:T(8,128)S(1)}, f32[1,1,8,128]{3,2,1,0:T(8,128)}, u32[]{:S(2)}) copy-start(f32[1,1,8,128]{3,2,1,0:T(8,128)} %param.18) | copy-start | bytes 12292
  2.0 0.7 %copy-start.6 = (f32[1,1,8,128]{3,2,1,0:T(8,128)S(1)}, f32[1,1,8,128]{3,2,1,0:T(8,128)}, u32[]{:S(2)}) copy-start(f32[1,1,8,128]{3,2,1,0:T(8,128)} %param.17) | copy-start | bytes 12292
  2.7 0.9 %copy-start = (f32[5,8,8,128]{3,2,1,0:T(8,128)S(1)}, f32[5,8,8,128]{3,2,1,0:T(8,128)}, u32[]{:S(2)}) copy-start(f32[5,8,8,128]{3,2,1,0:T(8,128)} %state.3) | copy-start | bytes 491524
  3.6 0.7 %copy-start.5 = (f32[3,1,1,8,128]{4,3,2,1,0:T(8,128)S(1)}, f32[3,1,1,8,128]{4,3,2,1,0:T(8,128)}, u32[]{:S(2)}) copy-start(f32[3,1,1,8,128]{4,3,2,1,0:T(8,128)} %param.16) | copy-start | bytes 36868
  4.3 0.7 %copy-start.8 = (s32[1,1,8,128]{3,2,1,0:T(8,128)S(1)}, s32[1,1,8,128]{3,2,1,0:T(8,128)}, u32[]{:S(2)}) copy-start(s32[1,1,8,128]{3,2,1,0:T(8,128)} %param.19) | copy-start | bytes 12292
  5.0 0.7 %copy-start.9 = (s32[1,1,8,128]{3,2,1,0:T(8,128)S(1)}, s32[1,1,8,128]{3,2,1,0:T(8,128)}, u32[]{:S(2)}) copy-start(s32[1,1,8,128]{3,2,1,0:T(8,128)} %param.20) | copy-start | bytes 12292
  5.7 0.7 %copy-start.10 = (s32[1,1,256]{2,1,0:T(1,128)S(1)}, s32[1,1,256]{2,1,0:T(1,128)}, u32[]{:S(2)}) copy-start(s32[1,1,256]{2,1,0:T(1,128)} %param.21) | copy-start | bytes 3076
  6.3 0.7 %copy-start.11 = (s32[1,1,256]{2,1,0:T(1,128)S(1)}, s32[1,1,256]{2,1,0:T(1,128)}, u32[]{:S(2)}) copy-start(s32[1,1,256]{2,1,0:T(1,128)} %param.23) | copy-start | bytes 3076
  7.0 0.7 %copy-start.12 = (s32[1,1,256]{2,1,0:T(1,128)S(1)}, s32[1,1,256]{2,1,0:T(1,128)}, u32[]{:S(2)}) copy-start(s32[1,1,256]{2,1,0:T(1,128)} %param.24) | copy-start | bytes 3076
  7.7 28.4 %copy-start.1 = (f32[5,8,8,128]{3,2,1,0:T(8,128)S(1)}, f32[5,8,8,128]{3,2,1,0:T(8,128)}, u32[]{:S(2)}) copy-start(f32[5,8,8,128]{3,2,1,0:T(8,128)} %state.3) | copy-start | bytes 491524
  7.7 28.4 %copy-start.3 = (f32[19,8,128]{2,1,0:T(8,128)S(1)}, f32[19,8,128]{2,1,0:T(8,128)}, u32[]{:S(2)}) copy-start(f32[19,8,128]{2,1,0:T(8,128)} %constant.4.clone.cols_ref) | copy-start | bytes 233476
  8.6 27.5 %copy-start.2 = (bf16[384,128]{1,0:T(8,128)(2,1)S(1)}, bf16[384,128]{1,0:T(8,128)(2,1)}, u32[]{:S(2)}) copy-start(bf16[384,128]{1,0:T(8,128)(2,1)} %constant.5.clone.mz) | copy-start | bytes 294916
  8.6 27.5 %all-to-all-start = ((f32[8,16,128]{2,1,0:T(8,128)}), f32[8,16,128]{2,1,0:T(8,128)S(1)}, u32[]{:S(2)}, u32[]{:S(2)}) async-start(f32[8,16,128]{2,1,0:T(8,128)} %get-tuple-element.25), calls=%async_computation | async-start | bytes 131072 | tf_op jit(solution)/shard_map/all_to_all | solution.py:472
  13.1 19.8 %collective-permute-start = (f32[5,8,128]{2,1,0:T(8,128)S(1)}, f32[5,8,128]{2,1,0:T(8,128)S(1)}, u32[]{:S(2)}, u32[]{:S(2)}) collective-permute-start(f32[5,8,128]{2,1,0:T(8,128)S(1)} %get-tuple-element.21), channel_id=1, source_target_pairs={{0,8},{8,16},{16,24},{24,32},{32,40},{40,48},{48,56},{56,64},{64,7... | collective-permute-start | bytes 61448 | tf_op jit(solution)/shard_map/ppermute | solution.py:413
  17.3 15.6 %collective-permute-start.1 = (f32[5,8,128]{2,1,0:T(8,128)S(1)}, f32[5,8,128]{2,1,0:T(8,128)S(1)}, u32[]{:S(2)}, u32[]{:S(2)}) collective-permute-start(f32[5,8,128]{2,1,0:T(8,128)S(1)} %get-tuple-element.22), channel_id=1, source_target_pairs={{8,0},{16,8},{24,16},{32,24},{40,32},{48,40},{56,48},{64,56},{72,6... | collective-permute-start | bytes 61448 | tf_op jit(solution)/shard_map/ppermute | solution.py:413
  29.5 3.5 %collective-permute-start.2 = (f32[5,8,128]{2,1,0:T(8,128)S(1)}, f32[5,8,128]{2,1,0:T(8,128)S(1)}, u32[]{:S(2)}, u32[]{:S(2)}) collective-permute-start(f32[5,8,128]{2,1,0:T(8,128)S(1)} %get-tuple-element.23), channel_id=1, source_target_pairs={{0,1},{1,2},{2,3},{3,4},{4,5},{5,6},{6,7},{8,9},{9,10},{10,11},{11... | collective-permute-start | bytes 61448 | tf_op jit(solution)/shard_map/ppermute | solution.py:413
  31.6 4.5 %collective-permute-start.3 = (f32[5,8,128]{2,1,0:T(8,128)S(1)}, f32[5,8,128]{2,1,0:T(8,128)S(1)}, u32[]{:S(2)}, u32[]{:S(2)}) collective-permute-start(f32[5,8,128]{2,1,0:T(8,128)S(1)} %get-tuple-element.24), channel_id=1, source_target_pairs={{1,0},{2,1},{3,2},{4,3},{5,4},{6,5},{7,6},{9,8},{10,9},{11,10},{12... | collective-permute-start | bytes 61448 | tf_op jit(solution)/shard_map/ppermute | solution.py:413
  37.4 16.2 %collective-permute-start.4 = (f32[9,8,128]{2,1,0:T(8,128)S(1)}, f32[9,8,128]{2,1,0:T(8,128)S(1)}, u32[]{:S(2)}, u32[]{:S(2)}) collective-permute-start(f32[9,8,128]{2,1,0:T(8,128)S(1)} %get-tuple-element.28), channel_id=1, source_target_pairs={{0,8},{8,16},{16,24},{24,32},{32,40},{40,48},{48,56},{56,64},{64,7... | collective-permute-start | bytes 110600 | tf_op jit(solution)/shard_map/ppermute | solution.py:413
  39.3 12.4 %collective-permute-start.5 = (f32[5,8,128]{2,1,0:T(8,128)S(1)}, f32[5,8,128]{2,1,0:T(8,128)S(1)}, u32[]{:S(2)}, u32[]{:S(2)}) collective-permute-start(f32[5,8,128]{2,1,0:T(8,128)S(1)} %get-tuple-element.29), channel_id=1, source_target_pairs={{8,0},{16,8},{24,16},{32,24},{40,32},{48,40},{56,48},{64,56},{72,6... | collective-permute-start | bytes 61448 | tf_op jit(solution)/shard_map/ppermute | solution.py:413
  46.6 5.2 %collective-permute-start.6 = (f32[5,8,128]{2,1,0:T(8,128)S(1)}, f32[5,8,128]{2,1,0:T(8,128)S(1)}, u32[]{:S(2)}, u32[]{:S(2)}) collective-permute-start(f32[5,8,128]{2,1,0:T(8,128)S(1)} %get-tuple-element.30), channel_id=1, source_target_pairs={{0,1},{1,2},{2,3},{3,4},{4,5},{5,6},{6,7},{8,9},{9,10},{10,11},{11... | collective-permute-start | bytes 61448 | tf_op jit(solution)/shard_map/ppermute | solution.py:413
  50.5 3.2 %collective-permute-start.7 = (f32[5,8,128]{2,1,0:T(8,128)S(1)}, f32[5,8,128]{2,1,0:T(8,128)S(1)}, u32[]{:S(2)}, u32[]{:S(2)}) collective-permute-start(f32[5,8,128]{2,1,0:T(8,128)S(1)} %get-tuple-element.31), channel_id=1, source_target_pairs={{1,0},{2,1},{3,2},{4,3},{5,4},{6,5},{7,6},{9,8},{10,9},{11,10},{12... | collective-permute-start | bytes 61448 | tf_op jit(solution)/shard_map/ppermute | solution.py:413
where the time goes:
time: 68.5 us; the launch traced here: 67.8 us
  starting transfers between devices  38.5 us (56%)
  blocking collectives  11.3 us (16%)
  local copies, waits for them, and re-layouts  5.72 us (8%)
  Pallas kernels  5.06 us (7%)
  waiting for transfers between devices  5.03 us (7%)
  between operations  2.11 us (3%)
    ppermute x8, starting transfers between devices, moved(): return lax.ppermute(block, axis, route)  34.1 us
    all_to_all x1, blocking collectives, local(): lax.all_to_all(back, 'cross', split_axis=0, concat_axis=0, tiled=True)  11.3 us
    unnamed x26, local copies, waits for them, and re-layouts  5.72 us
    ppermute x8, waiting for transfers between devices, moved(): return lax.ppermute(block, axis, route)  5.03 us
    all_to_all x1, starting transfers between devices, local(): lax.all_to_all(payload, 'cross', split_axis=0, concat_axis=0, tiled=True)  4.43 us
    pallas_call x1, Pallas kernels, local(): pl.pallas_call(second_kernel, out_shape=(shape(5, 8, 8, 128), shape(5, 8,...  2.21 us
  transfers between devices with their start and end apart: 9, of which 2 were waited for; matrix products, arithmetic and copies ran while one was open for 0% of the time, Pallas kernels for 0%

commit v1 on v0

--- a/solution.py
+++ b/solution.py
@@ -15,6 +15,7 @@
 
 TAU, LOAD, HOST, OUT_POS, IN_POS, IN_HOST, ALIVE = 6, 7, 8, 9, 10, 11, 12
 PLANES = 16
+FACE = 40
 
 
 def lgl_tables():
@@ -137,27 +138,48 @@
     return out_pos, landed[:8], landed[8:]
 
 
-def send_kernel(
-    state, xi, vel, tau, mass, host, alive, dep, dep_count, arr, arr_host, arr_count,
-    out, x_first, x_last, y_first, y_last,
-):
+def put_faces(out, state, first_row):
+    me = lax.axis_index("cross")
+    low, high = state[:, :, 0, :].reshape(FACE, 128), state[:, :, 7, :].reshape(FACE, 128)
+    for b in range(8):
+        out[b, pl.ds(first_row, FACE), :] = jnp.where(b > me, high, low)
+
+
+def take_faces(planes, first_row):
+    me, count = lax.axis_index("cross"), lax.axis_size("cross")
+    rows = pl.ds(first_row, FACE)
+    low = planes[pl.ds(jnp.maximum(me - 1, 0), 1), rows, :].reshape(5, 8, 128)
+    high = planes[pl.ds(jnp.minimum(me + 1, count - 1), 1), rows, :].reshape(5, 8, 128)
+    return jnp.where(me > 0, low, 0.0), jnp.where(me < count - 1, high, 0.0)
+
+
+def send_kernel(*refs):
+    dep_count, arr_count, sources = refs[0], refs[1], refs[2:12]
+    (out, x_first, x_last), held, sem = refs[12:15], refs[15:25], refs[25]
+    copies = [pltpu.make_async_copy(sources[k], held[k], sem.at[k]) for k in range(10)]
+    for copy in copies:
+        copy.start()
+    state, xi, vel, tau, mass, host, alive, dep, arr, arr_host = held
+    for copy in copies[7:]:
+        copy.wait()
+    out_pos, in_pos, in_host = list_planes(
+        dep[...], dep_count[...], arr[...], arr_host[...], arr_count[...]
+    )
+    out[:, OUT_POS, :] = out_pos
+    out[:, IN_POS, :] = in_pos
+    out[:, IN_HOST, :] = in_host
+    for copy in copies[:7]:
+        copy.wait()
     x_first[...] = state[:, 0]
     x_last[...] = state[:, 7]
-    y_first[...] = state[:, :, 0, :]
-    y_last[...] = state[:, :, 7, :]
+    put_faces(out, state, PLANES)
     live = alive[...].astype(F32)
-    out_pos, in_pos, in_host = list_planes(
-        dep[...], dep_count[0, 0], arr[...], arr_host[...], arr_count[0, 0]
-    )
     for a in range(3):
         out[:, a, :] = xi[a]
         out[:, 3 + a, :] = vel[a]
     out[:, TAU, :] = tau[...]
     out[:, LOAD, :] = mass[...] * live
     out[:, HOST, :] = host[...].astype(F32)
-    out[:, OUT_POS, :] = out_pos
-    out[:, IN_POS, :] = in_pos
-    out[:, IN_HOST, :] = in_host
     out[:, ALIVE, :] = live
     for r in range(ALIVE + 1, PLANES):
         out[:, r, :] = jnp.zeros((8, 128), F32)
@@ -232,7 +254,7 @@
     ]
 
 
-def fluid_rate(state, low_x, high_x, low_y, high_y, mean_flow, cols, mz):
+def inner_rate(state, mean_flow, cols, mz):
     q = [[state[v, i] for i in range(8)] for v in range(5)]
     both = jnp.concatenate([state[3].reshape(64, 128), state[4].reshape(64, 128)], axis=0)
     high, low = two_parts(both)
@@ -241,35 +263,32 @@
     node = lax.broadcasted_iota(jnp.int32, (8, 128), 1) & 7
     first, edge = node == 0, LIFT * flag((node == 0) | (node == 7))
     flow = [flux_x([q[v][i] for v in range(5)], mean_flow) for i in range(8)]
-    lows = [low_x[v] for v in range(5)]
-    highs = [high_x[v] for v in range(5)]
-    flow_low, flow_high = flux_x(lows, mean_flow), flux_x(highs, mean_flow)
-    first_y, last_y = cols[17], cols[18]
-    half_first, half_last = 0.5 * first_y, 0.5 * last_y
+    ends_y = cols[17] + cols[18]
+    half_y = 0.5 * (cols[18] - cols[17])
     result = [[None] * 8 for _ in range(5)]
     for i in range(8):
-        below = [row(low_y[v], i) for v in range(5)]
-        above = [row(high_y[v], i) for v in range(5)]
         slopes = {}
         for v in (2, 4):
             value = q[v][i]
-            slope = half_first * (below[v] - value) - half_last * (above[v] - value)
+            slope = half_y * value
             for j in range(8):
                 slope = slope + cols[8 + j] * row(value, j)
             slopes[v] = slope
         for v in range(5):
             value = q[v][i]
-            total = -float(DERIV[i, 0]) * flow[0][v]
-            for b in range(1, 8):
-                if DERIV[i, b] != 0.0:
-                    total = total - float(DERIV[i, b]) * flow[b][v]
+            factors = -DERIV[i]
             if i == 0:
-                total = total + (0.5 * LIFT) * (flow_low[v] - flow[0][v])
-                total = total - LIFT * (value - lows[v])
+                factors = factors - 0.5 * LIFT * (np.arange(8) == 0)
             if i == 7:
-                total = total - (0.5 * LIFT) * (flow_high[v] - flow[7][v])
-                total = total + LIFT * (highs[v] - value)
-            total = total + first_y * (below[v] - value) + last_y * (above[v] - value)
+                factors = factors + 0.5 * LIFT * (np.arange(8) == 7)
+            total = None
+            for b in range(8):
+                if factors[b] != 0.0:
+                    term = float(factors[b]) * flow[b][v]
+                    total = term if total is None else total + term
+            if i in (0, 7):
+                total = total - LIFT * value
+            total = total - ends_y * value
             if v in (0, 4):
                 total = total + slopes[2]
             if v == 2:
@@ -284,15 +303,38 @@
     return result
 
 
+def outer_rate(low_x, high_x, low_y, high_y, mean_flow, cols):
+    first_y, last_y = cols[17], cols[18]
+    lows, highs = [low_x[v] for v in range(5)], [high_x[v] for v in range(5)]
+    flow_low, flow_high = flux_x(lows, mean_flow), flux_x(highs, mean_flow)
+    result = [[None] * 8 for _ in range(5)]
+    for i in range(8):
+        below = [row(low_y[v], i) for v in range(5)]
+        above = [row(high_y[v], i) for v in range(5)]
+        flux = {0: 2, 2: 4, 4: 2}
+        for v in range(5):
+            at_first, at_last = below[v], above[v]
+            if v in flux:
+                at_first = at_first + 0.5 * below[flux[v]]
+                at_last = at_last - 0.5 * above[flux[v]]
+            total = first_y * at_first + last_y * at_last
+            if i == 0:
+                total = total + (0.5 * LIFT) * flow_low[v] + LIFT * lows[v]
+            if i == 7:
+                total = total - (0.5 * LIFT) * flow_high[v] + LIFT * highs[v]
+            result[v][i] = total
+    return result
+
+
 def droplets_first(planes, cols, w, l1, l2):
     for c in range(8):
-        block = planes[c]
+        block = planes[c, 0:PLANES]
         fill_weights(c, block[0:3], block[HOST : HOST + 1], cols, w, l1, l2)
 
 
 def first_kernel(
-    state, low_x, high_x, low_y, high_y, planes, cols_ref, mz,
-    state_out, reg_out, forward, x_first, y_first, y_last, drop_out,
+    state, low_x, high_x, planes, cols_ref, mz,
+    state_out, reg_out, forward, drop_out,
     w, s, l1, l2, fh, fl,
 ):
     cols = [cols_ref[t] for t in range(cols_ref.shape[0])]
@@ -302,7 +344,7 @@
     seat = lax.broadcasted_iota(jnp.int32, (128, 128), 0).astype(F32)
     records, seats = [], []
     for c in range(8):
-        block = planes[c]
+        block = planes[c, 0:PLANES]
         fluid = fluid_rows(c, s, l1, l2)
         accel = (fluid - block[3:6]) / block[TAU : TAU + 1]
         register = STEP_SIZE * accel
@@ -328,33 +370,33 @@
         forward[5 + 2 * g] = packed[0:8]
         forward[6 + 2 * g] = packed[8:16]
     source = deposit_all(w, fh, fl)
-    rate = fluid_rate(state, low_x, high_x, low_y, high_y, mean_flow, cols, mz)
+    low_y, high_y = take_faces(planes, PLANES)
+    rate = inner_rate(state, mean_flow, cols, mz)
+    extra = outer_rate(low_x, high_x, low_y, high_y, mean_flow, cols)
     for v in range(5):
         for i in range(8):
-            total = rate[v][i] + source[v - 1, i] if 1 <= v <= 3 else rate[v][i]
+            total = rate[v][i] + extra[v][i]
+            if 1 <= v <= 3:
+                total = total + source[v - 1, i]
             register = STEP_SIZE * total
             value = state[v, i] + COEF_B[0] * register
             reg_out[v, i] = register
             state_out[v, i] = value
-            y_first[v, pl.ds(i, 1), :] = value[0:1]
-            y_last[v, pl.ds(i, 1), :] = value[7:8]
-            if i == 0:
-                x_first[v] = value
             if i == 7:
                 forward[v] = value
 
 
-def second_kernel(
-    state, reg_in, low_x, high_x, low_y, high_y, planes, drops, cols_ref, mz,
-    state_out, reg_out, back,
-    w, s, l1, l2, fh, fl, held,
+def sample_kernel(
+    state, packed_in, planes, drops, cols_ref,
+    back, x_first, w, fh, fl,
+    s, l1, l2, held,
 ):
     cols = [cols_ref[t] for t in range(cols_ref.shape[0])]
     mean_flow = mean_profile(cols)
     seat = lax.broadcasted_iota(jnp.int32, (128, 128), 0).astype(F32)
     arrived = []
     for g in range(2):
-        packed = jnp.concatenate([low_x[5 + 2 * g], low_x[6 + 2 * g]], axis=0)
+        packed = jnp.concatenate([packed_in[5 + 2 * g], packed_in[6 + 2 * g]], axis=0)
         seats = []
         for c in range(4 * g, 4 * g + 4):
             in_pos = planes[c, IN_POS : IN_POS + 1]
@@ -363,7 +405,7 @@
         landed = dot_plain(three_parts(packed), jnp.concatenate(seats, axis=1))
         arrived.append(landed[0:16] + landed[16:32] + landed[32:48])
     for c in range(8):
-        block, drop = planes[c], drops[c]
+        block, drop = planes[c, 0:PLANES], drops[c]
         landed = arrived[c // 4][:, 128 * (c % 4) : 128 * (c % 4) + 128]
         stays = flag(block[OUT_POS : OUT_POS + 1] < 0.5)
         fresh = block[IN_POS : IN_POS + 1] > 0.5
@@ -388,11 +430,17 @@
         register = COEF_A[1] * block[3:6] + STEP_SIZE * accel
         velocity = block[0:3] + COEF_B[1] * register
         live = block[8:9]
-        back[c] = jnp.concatenate(
+        back[c, 0:8] = jnp.concatenate(
             [velocity * live, register * live, jnp.zeros((2, 128), F32)], axis=0
         )
+    put_faces(back, state, 8)
+    x_first[...] = state[:, 0]
+
+
+def inner_kernel(state, reg_in, w, fh, fl, cols_ref, mz, state_out, reg_out):
+    cols = [cols_ref[t] for t in range(cols_ref.shape[0])]
     source = deposit_all(w, fh, fl)
-    rate = fluid_rate(state, low_x, high_x, low_y, high_y, mean_flow, cols, mz)
+    rate = inner_rate(state, mean_profile(cols), cols, mz)
     for v in range(5):
         for i in range(8):
             total = rate[v][i] + source[v - 1, i] if 1 <= v <= 3 else rate[v][i]
@@ -401,10 +449,20 @@
             state_out[v, i] = state[v, i] + COEF_B[1] * register
 
 
-def last_kernel(returned, vel_out, reg_out):
+def last_kernel(
+    state, reg_in, low_x, high_x, returned, cols_ref, state_out, reg_out, vel_out, drop_out
+):
+    cols = [cols_ref[t] for t in range(cols_ref.shape[0])]
+    low_y, high_y = take_faces(returned, 8)
+    extra = outer_rate(low_x, high_x, low_y, high_y, mean_profile(cols), cols)
+    for v in range(5):
+        for i in range(8):
+            register = STEP_SIZE * extra[v][i]
+            reg_out[v, i] = reg_in[v, i] + register
+            state_out[v, i] = state[v, i] + COEF_B[1] * register
     for a in range(3):
         vel_out[a] = returned[:, a, :]
-        reg_out[a] = returned[:, 3 + a, :]
+        drop_out[a] = returned[:, 3 + a, :]
 
 
 def moved(block, axis, step):
@@ -418,16 +476,12 @@
 
 
 VMEM = pl.BlockSpec(memory_space=pltpu.VMEM)
-SMEM = pl.BlockSpec(memory_space=pltpu.SMEM)
+HBM = pl.BlockSpec(memory_space=pltpu.HBM)
 ROOM = pltpu.CompilerParams(vmem_limit_bytes=12 * 1024 * 1024)
-WORK = [
-    pltpu.VMEM((384, 1024), BF16),
-    pltpu.VMEM((192, 1024), F32),
-    pltpu.VMEM((8, 1024), F32),
-    pltpu.VMEM((8, 1024), F32),
-    pltpu.VMEM((192, 1024), BF16),
-    pltpu.VMEM((192, 1024), BF16),
-]
+FULL = pltpu.CompilerParams(vmem_limit_bytes=60 * 1024 * 1024)
+WEIGHTS = (384, 1024)
+FORCES = (192, 1024)
+WORK = [pltpu.VMEM((192, 1024), F32), pltpu.VMEM((8, 1024), F32), pltpu.VMEM((8, 1024), F32)]
 
 
 def local(
@@ -447,15 +501,8 @@
     lanes = depart_slots.shape[-1]
     cols = jnp.asarray(column_planes())
     mz = jnp.asarray(span_matrix())
-    face = shape(5, 8, 128)
-    payload, x_first, x_last, y_first, y_last = pl.pallas_call(
-        send_kernel,
-        out_shape=(shape(8, PLANES, 128), face, face, face, face),
-        in_specs=[VMEM] * 8 + [SMEM, VMEM, VMEM, SMEM],
-        out_specs=(VMEM,) * 5,
-        compiler_params=ROOM,
-        name="send",
-    )(
+    face, whole = shape(5, 8, 128), shape(5, 8, 8, 128)
+    arguments = (
         fluid_state,
         drop_xi.reshape(3, 8, 128),
         drop_vel.reshape(3, 8, 128),
@@ -464,51 +511,65 @@
         drop_host.reshape(8, 128),
         drop_alive.reshape(8, 128),
         depart_slots.reshape(1, lanes),
-        depart_count.reshape(1, 1),
         arrive_slots.reshape(1, lanes),
         arrive_host.reshape(1, lanes),
-        arrive_count.reshape(1, 1),
     )
+    counts = (depart_count.reshape(1, 1), arrive_count.reshape(1, 1))
+    payload, x_first, x_last = pl.pallas_call(
+        send_kernel,
+        out_shape=(shape(8, PLANES + FACE, 128), face, face),
+        in_specs=[VMEM] * 2 + [HBM] * 10,
+        out_specs=(VMEM,) * 3,
+        scratch_shapes=[pltpu.VMEM(a.shape, a.dtype) for a in arguments]
+        + [pltpu.SemaphoreType.DMA((10,))],
+        compiler_params=FULL,
+        name="send",
+    )(*counts, *arguments)
     planes = lax.all_to_all(payload, "cross", split_axis=0, concat_axis=0, tiled=True)
     low_x, high_x = moved(x_last, "stream", 1), moved(x_first, "stream", -1)
-    low_y, high_y = moved(y_last, "cross", 1), moved(y_first, "cross", -1)
-    state, register, forward, x_first, y_first, y_last, drops = pl.pallas_call(
+    state, register, forward, drops = pl.pallas_call(
         first_kernel,
-        out_shape=(
-            shape(5, 8, 8, 128),
-            shape(5, 8, 8, 128),
-            shape(9, 8, 128),
-            face,
-            face,
-            face,
-            shape(8, 8, 128),
-        ),
-        in_specs=[VMEM] * 8,
-        out_specs=(VMEM,) * 7,
-        scratch_shapes=WORK,
+        out_shape=(whole, whole, shape(9, 8, 128), shape(8, 8, 128)),
+        in_specs=[VMEM] * 6,
+        out_specs=(VMEM,) * 4,
+        scratch_shapes=[pltpu.VMEM(WEIGHTS, BF16)] + WORK + [pltpu.VMEM(FORCES, BF16)] * 2,
         compiler_params=ROOM,
         name="section_1",
-    )(fluid_state, low_x, high_x, low_y, high_y, planes, cols, mz)
-    low_x, high_x = moved(forward, "stream", 1), moved(x_first, "stream", -1)
-    low_y, high_y = moved(y_last, "cross", 1), moved(y_first, "cross", -1)
-    state, register, back = pl.pallas_call(
-        second_kernel,
-        out_shape=(shape(5, 8, 8, 128), shape(5, 8, 8, 128), shape(8, 8, 128)),
-        in_specs=[VMEM] * 10,
-        out_specs=(VMEM,) * 3,
+    )(fluid_state, low_x, high_x, planes, cols, mz)
+    low_x = moved(forward, "stream", 1)
+    back, x_first, w, fh, fl = pl.pallas_call(
+        sample_kernel,
+        out_shape=(
+            shape(8, 8 + FACE, 128),
+            face,
+            jax.ShapeDtypeStruct(WEIGHTS, BF16),
+            jax.ShapeDtypeStruct(FORCES, BF16),
+            jax.ShapeDtypeStruct(FORCES, BF16),
+        ),
+        in_specs=[VMEM] * 5,
+        out_specs=(VMEM,) * 5,
         scratch_shapes=WORK + [pltpu.VMEM((8, 16, 128), F32)],
         compiler_params=ROOM,
-        name="section_2",
-    )(state, register, low_x, high_x, low_y, high_y, planes, drops, cols, mz)
+        name="sample_2",
+    )(state, low_x, planes, drops, cols)
     returned = lax.all_to_all(back, "cross", split_axis=0, concat_axis=0, tiled=True)
-    velocity, drop_reg = pl.pallas_call(
+    high_x = moved(x_first, "stream", -1)
+    state, register = pl.pallas_call(
+        inner_kernel,
+        out_shape=(whole, whole),
+        in_specs=[VMEM] * 7,
+        out_specs=(VMEM,) * 2,
+        compiler_params=ROOM,
+        name="inner_2",
+    )(state, register, w, fh, fl, cols, mz)
+    state, register, velocity, drop_reg = pl.pallas_call(
         last_kernel,
-        out_shape=(shape(3, 8, 128), shape(3, 8, 128)),
-        in_specs=[VMEM],
-        out_specs=(VMEM, VMEM),
+        out_shape=(whole, whole, shape(3, 8, 128), shape(3, 8, 128)),
+        in_specs=[VMEM] * 6,
+        out_specs=(VMEM,) * 4,
         compiler_params=ROOM,
-        name="give",
-    )(returned)
+        name="last",
+    )(state, register, low_x, high_x, returned, cols)
     return (state, register, velocity.reshape(drop_vel.shape), drop_reg.reshape(drop_vel.shape))
 
 

time: 68.5 us -> 51.7 us (0.75)
  blocking collectives: 11.3 us -> 0 us
  starting transfers between devices: 38.5 us -> 31.5 us
  waiting for transfers between devices: 5.03 us -> 11.3 us
  local copies, waits for them, and re-layouts: 5.72 us -> 0.03 us
  Pallas kernels: 5.06 us -> 6.46 us
    ppermute x8 -> x4, starting transfers between devices: 34.1 us -> 22.2 us  [moved(): return lax.ppermute(block, axis, route)]
    all_to_all x1 -> x0, blocking collectives: 11.3 us -> none  [local(): lax.all_to_all(back, 'cross', split_axis=0, concat_axis=0, tiled=True)]
    unnamed x26 -> x10, local copies, waits for them, and re-layouts: 5.72 us -> 0.03 us
    ppermute x8 -> x4, waiting for transfers between devices: 5.03 us -> 10.1 us  [moved(): return lax.ppermute(block, axis, route)]
    all_to_all x0 -> x1, starting transfers between devices: none -> 4.8 us  [local(): lax.all_to_all(back, 'cross', split_axis=0, concat_axis=0, tiled=True)]
    pallas_call x4 -> x5, Pallas kernels: 5.06 us -> 6.46 us  [the longest x1 2.14 us: local(): pl.pallas_call(send_kernel, out_shape=(shape(8, PLANES + FACE, 128), face...]
    all_to_all x0 -> x1, waiting for transfers between devices: none -> 1.14 us  [local(): lax.all_to_all(back, 'cross', split_axis=0, concat_axis=0, tiled=True)]
  transfers between devices with their start and end apart: 9 -> 6, of which waited for: 2 -> 4; matrix products, arithmetic and copies ran while one was open for 0% -> 0% of each run, Pallas kernels for 0% -> 1%
where the time goes in v1:
time: 51.7 us; the launch traced here: 51.3 us
  starting transfers between devices  31.5 us (61%)
  waiting for transfers between devices  11.3 us (22%)
  Pallas kernels  6.46 us (12%)
  between operations  2.04 us (4%)
    ppermute x4, starting transfers between devices, moved(): return lax.ppermute(block, axis, route)  22.2 us
    ppermute x4, waiting for transfers between devices, moved(): return lax.ppermute(block, axis, route)  10.1 us
    all_to_all x1, starting transfers between devices, local(): lax.all_to_all(back, 'cross', split_axis=0, concat_axis=0, tiled=True)  4.8 us
    all_to_all x1, starting transfers between devices, local(): lax.all_to_all(payload, 'cross', split_axis=0, concat_axis=0, tiled=True)  4.44 us
    pallas_call x1, Pallas kernels, local(): pl.pallas_call(send_kernel, out_shape=(shape(8, PLANES + FACE, 128), face...  2.14 us
    pallas_call x1, Pallas kernels, local(): pl.pallas_call(sample_kernel, out_shape=(shape(8, 8 + FACE, 128), face, j...  1.65 us
    pallas_call x1, Pallas kernels, local(): pl.pallas_call(first_kernel, out_shape=(whole, whole, shape(9, 8, 128), s...  1.27 us
    all_to_all x1, waiting for transfers between devices, local(): lax.all_to_all(back, 'cross', split_axis=0, concat_axis=0, tiled=True)  1.14 us
  transfers between devices with their start and end apart: 6, of which 4 were waited for; matrix products, arithmetic and copies ran while one was open for 0% of the time, Pallas kernels for 1%

profile of v1, /device:TPU:32, one launch (start us, length us, event | category | flops | bytes accessed | tf_op | source)
XLA Modules:
  0.0 51.3 jit_solution(894154858971184680)
XLA Ops:
  1.9 2.1 %send.1 = (f32[8,56,128]{2,1,0:T(8,128)}, f32[5,8,128]{2,1,0:T(8,128)}, f32[5,8,128]{2,1,0:T(8,128)}) custom-call(s32[1,1]{1,0:T(1,128)S(6)} %copy.20.refs_0_, s32[1,1]{1,0:T(1,128)S(6)} %copy.21.refs_1_, f32[5,8,8,128]{3,2,1,0:T(8,128)} %state.1, f32[3,8,128]{2,1,0:T(8,128)} %bitcast.15, f32[3,8,128]{2,1,0:T(8,128)} %bitcast.16, f32[8,128]{1,0:T(8,128)} %bitcast.17, ...), custom_call_target="tpu_custom_call" | custom-call | tf_op jit(solution)/shard_map/send/pallas_call | solution.py:518
  4.1 0.0 copy-start.4
  4.1 0.0 copy-start.3
  4.1 0.0 copy-start
  4.1 0.0 copy-start.1
  4.1 0.0 copy-start.2
  4.1 4.4 %all-to-all-start = ((f32[8,56,128]{2,1,0:T(8,128)}), f32[8,56,128]{2,1,0:T(8,128)S(1)}, u32[]{:S(2)}, u32[]{:S(2)}) async-start(f32[8,56,128]{2,1,0:T(8,128)} %get-tuple-element.24), calls=%async_computation | async-start | bytes 458752 | tf_op jit(solution)/shard_map/all_to_all | solution.py:528
  8.6 0.0 copy-done.4
  8.6 4.3 %collective-permute-start = (f32[5,8,128]{2,1,0:T(8,128)S(1)}, f32[5,8,128]{2,1,0:T(8,128)S(1)}, u32[]{:S(2)}, u32[]{:S(2)}) collective-permute-start(f32[5,8,128]{2,1,0:T(8,128)S(1)} %copy-done.4), channel_id=1, source_target_pairs={{0,8},{8,16},{16,24},{24,32},{32,40},{40,48},{48,56},{56,64},{64,7... | collective-permute-start | bytes 61448 | tf_op jit(solution)/shard_map/ppermute | solution.py:471
  12.9 0.0 copy-done.3
  12.9 12.1 %collective-permute-start.1 = (f32[5,8,128]{2,1,0:T(8,128)S(1)}, f32[5,8,128]{2,1,0:T(8,128)S(1)}, u32[]{:S(2)}, u32[]{:S(2)}) collective-permute-start(f32[5,8,128]{2,1,0:T(8,128)S(1)} %copy-done.3), channel_id=1, source_target_pairs={{8,0},{16,8},{24,16},{32,24},{40,32},{48,40},{56,48},{64,56},{72,6... | collective-permute-start | bytes 61448 | tf_op jit(solution)/shard_map/ppermute | solution.py:471
  25.0 0.0 collective-permute-done.low_x
  25.0 1.4 %collective-permute-done.1.high_x = f32[5,8,128]{2,1,0:T(8,128)S(1)} collective-permute-done((f32[5,8,128]{2,1,0:T(8,128)S(1)}, f32[5,8,128]{2,1,0:T(8,128)S(1)}, u32[]{:S(2)}, u32[]{:S(2)}) %collective-permute-start.1) | collective-permute-done | bytes 20512 | tf_op jit(solution)/shard_map/ppermute | solution.py:471
  26.5 0.0 all-to-all-done.planes
  26.5 0.0 copy-done
  26.5 0.0 copy-done.1
  26.5 0.0 copy-done.2
  26.5 1.3 %section_1.1 = (f32[5,8,8,128]{3,2,1,0:T(8,128)S(1)}, f32[5,8,8,128]{3,2,1,0:T(8,128)S(1)}, f32[9,8,128]{2,1,0:T(8,128)S(1)}, f32[8,8,128]{2,1,0:T(8,128)S(1)}) custom-call(f32[5,8,8,128]{3,2,1,0:T(8,128)S(1)} %copy-done.1, f32[5,8,128]{2,1,0:T(8,128)S(1)} %collective-permute-done.low_x, f32[5,8,128]{2,1,0:T(8,128)S(1)} %collective-permute-done.1.high_x, ...), custom_call_target="tpu_custom_call" | custom-call | tf_op jit(solution)/shard_map/section_1/pallas_call | solution.py:530
  27.8 1.9 %collective-permute-start.2 = (f32[9,8,128]{2,1,0:T(8,128)S(1)}, f32[9,8,128]{2,1,0:T(8,128)S(1)}, u32[]{:S(2)}, u32[]{:S(2)}) collective-permute-start(f32[9,8,128]{2,1,0:T(8,128)S(1)} %get-tuple-element.27), channel_id=1, source_target_pairs={{0,8},{8,16},{16,24},{24,32},{32,40},{40,48},{48,56},{56,64},{64,7... | collective-permute-start | bytes 110600 | tf_op jit(solution)/shard_map/ppermute | solution.py:471
  29.7 7.5 %collective-permute-done.2.packed_in.low_x = f32[9,8,128]{2,1,0:T(8,128)S(1)} collective-permute-done((f32[9,8,128]{2,1,0:T(8,128)S(1)}, f32[9,8,128]{2,1,0:T(8,128)S(1)}, u32[]{:S(2)}, u32[]{:S(2)}) %collective-permute-start.2) | collective-permute-done | bytes 36896 | tf_op jit(solution)/shard_map/ppermute | solution.py:471
  37.2 1.7 %sample_2.1 = (f32[8,48,128]{2,1,0:T(8,128)}, f32[5,8,128]{2,1,0:T(8,128)S(1)}, bf16[384,1024]{1,0:T(8,128)(2,1)S(1)}, bf16[192,1024]{1,0:T(8,128)(2,1)S(1)}, bf16[192,1024]{1,0:T(8,128)(2,1)S(1)}) custom-call(f32[5,8,8,128]{3,2,1,0:T(8,128)S(1)} %get-tuple-element.25.state, f32[9,8,128]{2,1,0:T(8,128)S(1)} %collective-permute-done.2.packed_in.low_x, ...), custom_call_target="tpu_custom_call" | custom-call | tf_op jit(solution)/shard_map/sample_2/pallas_call | solution.py:540
  38.9 4.8 %all-to-all-start.1 = ((f32[8,48,128]{2,1,0:T(8,128)}), f32[8,48,128]{2,1,0:T(8,128)S(1)}, u32[]{:S(2)}, u32[]{:S(2)}) async-start(f32[8,48,128]{2,1,0:T(8,128)} %get-tuple-element.35), calls=%async_computation.1 | async-start | bytes 393216 | tf_op jit(solution)/shard_map/all_to_all | solution.py:555
  43.7 3.9 %collective-permute-start.3 = (f32[5,8,128]{2,1,0:T(8,128)S(1)}, f32[5,8,128]{2,1,0:T(8,128)S(1)}, u32[]{:S(2)}, u32[]{:S(2)}) collective-permute-start(f32[5,8,128]{2,1,0:T(8,128)S(1)} %get-tuple-element.34), channel_id=1, source_target_pairs={{8,0},{16,8},{24,16},{32,24},{40,32},{48,40},{56,48},{64,56},{72,6... | collective-permute-start | bytes 61448 | tf_op jit(solution)/shard_map/ppermute | solution.py:471
  47.6 0.6 %inner_2.1 = (f32[5,8,8,128]{3,2,1,0:T(8,128)S(1)}, f32[5,8,8,128]{3,2,1,0:T(8,128)S(1)}) custom-call(f32[5,8,8,128]{3,2,1,0:T(8,128)S(1)} %get-tuple-element.25.state, f32[5,8,8,128]{3,2,1,0:T(8,128)S(1)} %get-tuple-element.26.reg_in, bf16[384,1024]{1,0:T(8,128)(2,1)S(1)} %get-tuple-element.29.w, bf16[192,1024]{1,0:T(8,128)(2,1)S(1)} %get-tuple-element.30.fh, ...), custom_call_target="tpu_custom_call" | custom-call | tf_op jit(solution)/shard_map/inner_2/pallas_call | solution.py:557
  48.2 1.2 %collective-permute-done.3.high_x = f32[5,8,128]{2,1,0:T(8,128)S(1)} collective-permute-done((f32[5,8,128]{2,1,0:T(8,128)S(1)}, f32[5,8,128]{2,1,0:T(8,128)S(1)}, u32[]{:S(2)}, u32[]{:S(2)}) %collective-permute-start.3) | collective-permute-done | bytes 20512 | tf_op jit(solution)/shard_map/ppermute | solution.py:471
  49.3 1.1 %all-to-all-done.1.returned = f32[8,48,128]{2,1,0:T(8,128)S(1)} async-done(((f32[8,48,128]{2,1,0:T(8,128)}), f32[8,48,128]{2,1,0:T(8,128)S(1)}, u32[]{:S(2)}, u32[]{:S(2)}) %all-to-all-start.1) | async-done | bytes 196640 | tf_op jit(solution)/shard_map/all_to_all | solution.py:555
  50.5 0.8 %last.1 = (f32[5,8,8,128]{3,2,1,0:T(8,128)}, f32[5,8,8,128]{3,2,1,0:T(8,128)}, f32[3,8,128]{2,1,0:T(8,128)}, f32[3,8,128]{2,1,0:T(8,128)}) custom-call(f32[5,8,8,128]{3,2,1,0:T(8,128)S(1)} %get-tuple-element.32.state, f32[5,8,8,128]{3,2,1,0:T(8,128)S(1)} %get-tuple-element.33.reg_in, f32[9,8,128]{2,1,0:T(8,128)S(1)} %collective-permute-done.2.packed_in.low_x, ...), custom_call_target="tpu_custom_call" | custom-call | tf_op jit(solution)/shard_map/last/pallas_call | solution.py:565
Async XLA Ops:
  4.1 4.5 %copy-start.4 = (f32[5,8,128]{2,1,0:T(8,128)S(1)}, f32[5,8,128]{2,1,0:T(8,128)}, u32[]{:S(2)}) copy-start(f32[5,8,128]{2,1,0:T(8,128)} %get-tuple-element.22) | copy-start | bytes 61444
  4.1 8.8 %copy-start.3 = (f32[5,8,128]{2,1,0:T(8,128)S(1)}, f32[5,8,128]{2,1,0:T(8,128)}, u32[]{:S(2)}) copy-start(f32[5,8,128]{2,1,0:T(8,128)} %get-tuple-element.23) | copy-start | bytes 61444
  4.1 22.4 %copy-start = (f32[19,8,128]{2,1,0:T(8,128)S(1)}, f32[19,8,128]{2,1,0:T(8,128)}, u32[]{:S(2)}) copy-start(f32[19,8,128]{2,1,0:T(8,128)} %constant.4.clone.cols_ref) | copy-start | bytes 233476
  4.1 22.4 %copy-start.1 = (f32[5,8,8,128]{3,2,1,0:T(8,128)S(1)}, f32[5,8,8,128]{3,2,1,0:T(8,128)}, u32[]{:S(2)}) copy-start(f32[5,8,8,128]{3,2,1,0:T(8,128)} %state.1) | copy-start | bytes 491524
  4.1 22.4 %copy-start.2 = (bf16[384,128]{1,0:T(8,128)(2,1)S(1)}, bf16[384,128]{1,0:T(8,128)(2,1)}, u32[]{:S(2)}) copy-start(bf16[384,128]{1,0:T(8,128)(2,1)} %constant.5.clone.mz) | copy-start | bytes 294916
  4.1 22.3 %all-to-all-start = ((f32[8,56,128]{2,1,0:T(8,128)}), f32[8,56,128]{2,1,0:T(8,128)S(1)}, u32[]{:S(2)}, u32[]{:S(2)}) async-start(f32[8,56,128]{2,1,0:T(8,128)} %get-tuple-element.24), calls=%async_computation | async-start | bytes 458752 | tf_op jit(solution)/shard_map/all_to_all | solution.py:528
  8.6 16.4 %collective-permute-start = (f32[5,8,128]{2,1,0:T(8,128)S(1)}, f32[5,8,128]{2,1,0:T(8,128)S(1)}, u32[]{:S(2)}, u32[]{:S(2)}) collective-permute-start(f32[5,8,128]{2,1,0:T(8,128)S(1)} %copy-done.4), channel_id=1, source_target_pairs={{0,8},{8,16},{16,24},{24,32},{32,40},{40,48},{48,56},{56,64},{64,7... | collective-permute-start | bytes 61448 | tf_op jit(solution)/shard_map/ppermute | solution.py:471
  12.9 13.6 %collective-permute-start.1 = (f32[5,8,128]{2,1,0:T(8,128)S(1)}, f32[5,8,128]{2,1,0:T(8,128)S(1)}, u32[]{:S(2)}, u32[]{:S(2)}) collective-permute-start(f32[5,8,128]{2,1,0:T(8,128)S(1)} %copy-done.3), channel_id=1, source_target_pairs={{8,0},{16,8},{24,16},{32,24},{40,32},{48,40},{56,48},{64,56},{72,6... | collective-permute-start | bytes 61448 | tf_op jit(solution)/shard_map/ppermute | solution.py:471
  27.8 9.5 %collective-permute-start.2 = (f32[9,8,128]{2,1,0:T(8,128)S(1)}, f32[9,8,128]{2,1,0:T(8,128)S(1)}, u32[]{:S(2)}, u32[]{:S(2)}) collective-permute-start(f32[9,8,128]{2,1,0:T(8,128)S(1)} %get-tuple-element.27), channel_id=1, source_target_pairs={{0,8},{8,16},{16,24},{24,32},{32,40},{40,48},{48,56},{56,64},{64,7... | collective-permute-start | bytes 110600 | tf_op jit(solution)/shard_map/ppermute | solution.py:471
  38.9 11.6 %all-to-all-start.1 = ((f32[8,48,128]{2,1,0:T(8,128)}), f32[8,48,128]{2,1,0:T(8,128)S(1)}, u32[]{:S(2)}, u32[]{:S(2)}) async-start(f32[8,48,128]{2,1,0:T(8,128)} %get-tuple-element.35), calls=%async_computation.1 | async-start | bytes 393216 | tf_op jit(solution)/shard_map/all_to_all | solution.py:555
  43.7 5.7 %collective-permute-start.3 = (f32[5,8,128]{2,1,0:T(8,128)S(1)}, f32[5,8,128]{2,1,0:T(8,128)S(1)}, u32[]{:S(2)}, u32[]{:S(2)}) collective-permute-start(f32[5,8,128]{2,1,0:T(8,128)S(1)} %get-tuple-element.34), channel_id=1, source_target_pairs={{8,0},{16,8},{24,16},{32,24},{40,32},{48,40},{56,48},{64,56},{72,6... | collective-permute-start | bytes 61448 | tf_op jit(solution)/shard_map/ppermute | solution.py:471

commit v2 on v1

--- a/solution.py
+++ b/solution.py
@@ -155,7 +155,7 @@
 
 def send_kernel(*refs):
     dep_count, arr_count, sources = refs[0], refs[1], refs[2:12]
-    (out, x_first, x_last), held, sem = refs[12:15], refs[15:25], refs[25]
+    (out, x_first), held, sem = refs[12:14], refs[14:24], refs[24]
     copies = [pltpu.make_async_copy(sources[k], held[k], sem.at[k]) for k in range(10)]
     for copy in copies:
         copy.start()
@@ -171,7 +171,6 @@
     for copy in copies[:7]:
         copy.wait()
     x_first[...] = state[:, 0]
-    x_last[...] = state[:, 7]
     put_faces(out, state, PLANES)
     live = alive[...].astype(F32)
     for a in range(3):
@@ -303,26 +302,29 @@
     return result
 
 
-def outer_rate(low_x, high_x, low_y, high_y, mean_flow, cols):
+def lift_first(face, mean_flow):
+    flow = flux_x(face, mean_flow)
+    return [(0.5 * LIFT) * flow[v] + LIFT * face[v] for v in range(5)]
+
+
+def lift_last(face, mean_flow):
+    flow = flux_x(face, mean_flow)
+    return [LIFT * face[v] - (0.5 * LIFT) * flow[v] for v in range(5)]
+
+
+def lifts_y(low_y, high_y, cols):
     first_y, last_y = cols[17], cols[18]
-    lows, highs = [low_x[v] for v in range(5)], [high_x[v] for v in range(5)]
-    flow_low, flow_high = flux_x(lows, mean_flow), flux_x(highs, mean_flow)
+    flux = {0: 2, 2: 4, 4: 2}
     result = [[None] * 8 for _ in range(5)]
     for i in range(8):
         below = [row(low_y[v], i) for v in range(5)]
         above = [row(high_y[v], i) for v in range(5)]
-        flux = {0: 2, 2: 4, 4: 2}
         for v in range(5):
             at_first, at_last = below[v], above[v]
             if v in flux:
                 at_first = at_first + 0.5 * below[flux[v]]
                 at_last = at_last - 0.5 * above[flux[v]]
-            total = first_y * at_first + last_y * at_last
-            if i == 0:
-                total = total + (0.5 * LIFT) * flow_low[v] + LIFT * lows[v]
-            if i == 7:
-                total = total - (0.5 * LIFT) * flow_high[v] + LIFT * highs[v]
-            result[v][i] = total
+            result[v][i] = first_y * at_first + last_y * at_last
     return result
 
 
@@ -333,7 +335,7 @@
 
 
 def first_kernel(
-    state, low_x, high_x, planes, cols_ref, mz,
+    state, rate, planes, cols_ref,
     state_out, reg_out, forward, drop_out,
     w, s, l1, l2, fh, fl,
 ):
@@ -367,15 +369,15 @@
             jnp.concatenate(seats[group], axis=1),
         )
         packed = packed[0:16] + packed[16:32] + packed[32:48]
-        forward[5 + 2 * g] = packed[0:8]
-        forward[6 + 2 * g] = packed[8:16]
+        forward[10 + 2 * g] = packed[0:8]
+        forward[11 + 2 * g] = packed[8:16]
     source = deposit_all(w, fh, fl)
     low_y, high_y = take_faces(planes, PLANES)
-    rate = inner_rate(state, mean_flow, cols, mz)
-    extra = outer_rate(low_x, high_x, low_y, high_y, mean_flow, cols)
+    extra = lifts_y(low_y, high_y, cols)
     for v in range(5):
+        forward[v] = state[v, 7]
         for i in range(8):
-            total = rate[v][i] + extra[v][i]
+            total = rate[v, i] + extra[v][i]
             if 1 <= v <= 3:
                 total = total + source[v - 1, i]
             register = STEP_SIZE * total
@@ -383,20 +385,33 @@
             reg_out[v, i] = register
             state_out[v, i] = value
             if i == 7:
-                forward[v] = value
+                forward[5 + v] = value
 
 
 def sample_kernel(
-    state, packed_in, planes, drops, cols_ref,
-    back, x_first, w, fh, fl,
-    s, l1, l2, held,
+    state_in, reg_in, behind, ahead, planes, drops, cols_ref,
+    state, reg, back, x_first, w, l1, l2, force,
+    s, held,
 ):
     cols = [cols_ref[t] for t in range(cols_ref.shape[0])]
     mean_flow = mean_profile(cols)
+    lifts = {
+        0: lift_first([behind[v] for v in range(5)], mean_flow),
+        7: lift_last([ahead[v] for v in range(5)], mean_flow),
+    }
+    for v in range(5):
+        for i in range(8):
+            if i in lifts:
+                register = STEP_SIZE * lifts[i][v]
+                reg[v, i] = reg_in[v, i] + register
+                state[v, i] = state_in[v, i] + COEF_B[0] * register
+            else:
+                reg[v, i] = reg_in[v, i]
+                state[v, i] = state_in[v, i]
     seat = lax.broadcasted_iota(jnp.int32, (128, 128), 0).astype(F32)
     arrived = []
     for g in range(2):
-        packed = jnp.concatenate([packed_in[5 + 2 * g], packed_in[6 + 2 * g]], axis=0)
+        packed = jnp.concatenate([behind[10 + 2 * g], behind[11 + 2 * g]], axis=0)
         seats = []
         for c in range(4 * g, 4 * g + 4):
             in_pos = planes[c, IN_POS : IN_POS + 1]
@@ -426,7 +441,7 @@
         block = held[c]
         fluid = fluid_rows(c, s, l1, l2)
         accel = (fluid - block[0:3]) / block[6:7]
-        fill_force(c, accel * block[7:8], l1, l2, fh, fl)
+        force[c, 0:3] = accel * block[7:8]
         register = COEF_A[1] * block[3:6] + STEP_SIZE * accel
         velocity = block[0:3] + COEF_B[1] * register
         live = block[8:9]
@@ -437,27 +452,45 @@
     x_first[...] = state[:, 0]
 
 
-def inner_kernel(state, reg_in, w, fh, fl, cols_ref, mz, state_out, reg_out):
+def rate_kernel(state, cols_ref, mz, rate_out):
     cols = [cols_ref[t] for t in range(cols_ref.shape[0])]
-    source = deposit_all(w, fh, fl)
     rate = inner_rate(state, mean_profile(cols), cols, mz)
     for v in range(5):
         for i in range(8):
+            rate_out[v, i] = rate[v][i]
+
+
+def inner_kernel(
+    state, reg_in, start, behind, w, l1, l2, force, cols_ref, mz, state_out, reg_out, fh, fl
+):
+    cols = [cols_ref[t] for t in range(cols_ref.shape[0])]
+    mean_flow = mean_profile(cols)
+    added = lift_last([start[v, 0] for v in range(5)], mean_flow)
+    factor = jnp.where(lax.axis_index("stream") > 0, STEP_SIZE * COEF_B[0], 0.0)
+    lifts = {0: lift_first([behind[5 + v] + factor * added[v] for v in range(5)], mean_flow)}
+    for c in range(8):
+        fill_force(c, force[c, 0:3], l1, l2, fh, fl)
+    source = deposit_all(w, fh, fl)
+    rate = inner_rate(state, mean_flow, cols, mz)
+    for v in range(5):
+        for i in range(8):
             total = rate[v][i] + source[v - 1, i] if 1 <= v <= 3 else rate[v][i]
+            if i in lifts:
+                total = total + lifts[i][v]
             register = COEF_A[1] * reg_in[v, i] + STEP_SIZE * total
             reg_out[v, i] = register
             state_out[v, i] = state[v, i] + COEF_B[1] * register
 
 
-def last_kernel(
-    state, reg_in, low_x, high_x, returned, cols_ref, state_out, reg_out, vel_out, drop_out
-):
+def last_kernel(state, reg_in, ahead, returned, cols_ref, state_out, reg_out, vel_out, drop_out):
     cols = [cols_ref[t] for t in range(cols_ref.shape[0])]
     low_y, high_y = take_faces(returned, 8)
-    extra = outer_rate(low_x, high_x, low_y, high_y, mean_profile(cols), cols)
+    extra = lifts_y(low_y, high_y, cols)
+    lifts = {7: lift_last([ahead[v] for v in range(5)], mean_profile(cols))}
     for v in range(5):
         for i in range(8):
-            register = STEP_SIZE * extra[v][i]
+            total = extra[v][i] + lifts[i][v] if i in lifts else extra[v][i]
+            register = STEP_SIZE * total
             reg_out[v, i] = reg_in[v, i] + register
             state_out[v, i] = state[v, i] + COEF_B[1] * register
     for a in range(3):
@@ -515,61 +548,73 @@
         arrive_host.reshape(1, lanes),
     )
     counts = (depart_count.reshape(1, 1), arrive_count.reshape(1, 1))
-    payload, x_first, x_last = pl.pallas_call(
+    payload, x_first = pl.pallas_call(
         send_kernel,
-        out_shape=(shape(8, PLANES + FACE, 128), face, face),
+        out_shape=(shape(8, PLANES + FACE, 128), face),
         in_specs=[VMEM] * 2 + [HBM] * 10,
-        out_specs=(VMEM,) * 3,
+        out_specs=(VMEM, VMEM),
         scratch_shapes=[pltpu.VMEM(a.shape, a.dtype) for a in arguments]
         + [pltpu.SemaphoreType.DMA((10,))],
         compiler_params=FULL,
         name="send",
     )(*counts, *arguments)
     planes = lax.all_to_all(payload, "cross", split_axis=0, concat_axis=0, tiled=True)
-    low_x, high_x = moved(x_last, "stream", 1), moved(x_first, "stream", -1)
+    ahead = moved(x_first, "stream", -1)
+    rate = pl.pallas_call(
+        rate_kernel,
+        out_shape=whole,
+        in_specs=[VMEM] * 3,
+        out_specs=VMEM,
+        compiler_params=ROOM,
+        name="inner_1",
+    )(fluid_state, cols, mz)
     state, register, forward, drops = pl.pallas_call(
         first_kernel,
-        out_shape=(whole, whole, shape(9, 8, 128), shape(8, 8, 128)),
-        in_specs=[VMEM] * 6,
+        out_shape=(whole, whole, shape(14, 8, 128), shape(8, 8, 128)),
+        in_specs=[VMEM] * 4,
         out_specs=(VMEM,) * 4,
         scratch_shapes=[pltpu.VMEM(WEIGHTS, BF16)] + WORK + [pltpu.VMEM(FORCES, BF16)] * 2,
         compiler_params=ROOM,
         name="section_1",
-    )(fluid_state, low_x, high_x, planes, cols, mz)
-    low_x = moved(forward, "stream", 1)
-    back, x_first, w, fh, fl = pl.pallas_call(
+    )(fluid_state, rate, planes, cols)
+    behind = moved(forward, "stream", 1)
+    state, register, back, x_first, w, l1, l2, force = pl.pallas_call(
         sample_kernel,
         out_shape=(
+            whole,
+            whole,
             shape(8, 8 + FACE, 128),
             face,
             jax.ShapeDtypeStruct(WEIGHTS, BF16),
-            jax.ShapeDtypeStruct(FORCES, BF16),
-            jax.ShapeDtypeStruct(FORCES, BF16),
+            shape(8, 1024),
+            shape(8, 1024),
+            shape(8, 8, 128),
         ),
-        in_specs=[VMEM] * 5,
-        out_specs=(VMEM,) * 5,
-        scratch_shapes=WORK + [pltpu.VMEM((8, 16, 128), F32)],
+        in_specs=[VMEM] * 7,
+        out_specs=(VMEM,) * 8,
+        scratch_shapes=WORK[:1] + [pltpu.VMEM((8, 16, 128), F32)],
         compiler_params=ROOM,
         name="sample_2",
-    )(state, low_x, planes, drops, cols)
+    )(state, register, behind, ahead, planes, drops, cols)
     returned = lax.all_to_all(back, "cross", split_axis=0, concat_axis=0, tiled=True)
-    high_x = moved(x_first, "stream", -1)
+    ahead = moved(x_first, "stream", -1)
     state, register = pl.pallas_call(
         inner_kernel,
         out_shape=(whole, whole),
-        in_specs=[VMEM] * 7,
+        in_specs=[VMEM] * 10,
         out_specs=(VMEM,) * 2,
+        scratch_shapes=[pltpu.VMEM(FORCES, BF16)] * 2,
         compiler_params=ROOM,
         name="inner_2",
-    )(state, register, w, fh, fl, cols, mz)
+    )(state, register, fluid_state, behind, w, l1, l2, force, cols, mz)
     state, register, velocity, drop_reg = pl.pallas_call(
         last_kernel,
         out_shape=(whole, whole, shape(3, 8, 128), shape(3, 8, 128)),
-        in_specs=[VMEM] * 6,
+        in_specs=[VMEM] * 5,
         out_specs=(VMEM,) * 4,
         compiler_params=ROOM,
         name="last",
-    )(state, register, low_x, high_x, returned, cols)
+    )(state, register, ahead, returned, cols)
     return (state, register, velocity.reshape(drop_vel.shape), drop_reg.reshape(drop_vel.shape))
 
 

time: 51.7 us -> 50.2 us (0.971)
  the two profiles are of different devices: /device:TPU:32 before, /device:TPU:34 now
where the time goes in v2:
time: 50.2 us; the launch traced here: 49.8 us
  starting transfers between devices  33.6 us (67%)
  waiting for transfers between devices  7.68 us (15%)
  Pallas kernels  6.42 us (13%)
  between operations  2.03 us (4%)
    ppermute x3, starting transfers between devices, moved(): return lax.ppermute(block, axis, route)  23.9 us
    all_to_all x1, waiting for transfers between devices, local(): lax.all_to_all(payload, 'cross', split_axis=0, concat_axis=0, tiled=True)  5.44 us
    all_to_all x1, starting transfers between devices, local(): lax.all_to_all(payload, 'cross', split_axis=0, concat_axis=0, tiled=True)  4.97 us
    all_to_all x1, starting transfers between devices, local(): lax.all_to_all(back, 'cross', split_axis=0, concat_axis=0, tiled=True)  4.75 us
    ppermute x3, waiting for transfers between devices, moved(): return lax.ppermute(block, axis, route)  2.24 us
    pallas_call x1, Pallas kernels, local(): pl.pallas_call(send_kernel, out_shape=(shape(8, PLANES + FACE, 128), face...  2.13 us
    pallas_call x1, Pallas kernels, local(): pl.pallas_call(sample_kernel, out_shape=(whole, whole, shape(8, 8 + FACE,...  1.53 us
    pallas_call x1, Pallas kernels, local(): pl.pallas_call(first_kernel, out_shape=(whole, whole, shape(14, 8, 128),...  1.04 us
  transfers between devices with their start and end apart: 5, of which 3 were waited for; matrix products, arithmetic and copies ran while one was open for 0% of the time, Pallas kernels for 2%

profile of v2, /device:TPU:34, one launch (start us, length us, event | category | flops | bytes accessed | tf_op | source)
XLA Modules:
  0.0 49.8 jit_solution(12957786630682017197)
XLA Ops:
  1.9 2.1 %send.1 = (f32[8,56,128]{2,1,0:T(8,128)}, f32[5,8,128]{2,1,0:T(8,128)}) custom-call(s32[1,1]{1,0:T(1,128)S(6)} %copy.20.refs_0_, s32[1,1]{1,0:T(1,128)S(6)} %copy.21.refs_1_, f32[5,8,8,128]{3,2,1,0:T(8,128)} %start.1, f32[3,8,128]{2,1,0:T(8,128)} %bitcast.15, f32[3,8,128]{2,1,0:T(8,128)} %bitcast.16, f32[8,128]{1,0:T(8,128)} %bitcast.17, f32[8,128]{1,0:T(8,128)} %bitcast.18, ...), custom_call_target="tpu_custom_call" | custom-call | tf_op jit(solution)/shard_map/send/pallas_call | solution.py:551
  4.1 0.0 copy-start
  4.1 0.0 copy-start.1
  4.1 0.0 copy-start.2
  4.1 5.0 %all-to-all-start = ((f32[8,56,128]{2,1,0:T(8,128)}), f32[8,56,128]{2,1,0:T(8,128)S(1)}, u32[]{:S(2)}, u32[]{:S(2)}) async-start(f32[8,56,128]{2,1,0:T(8,128)} %get-tuple-element.24), calls=%async_computation | async-start | bytes 458752 | tf_op jit(solution)/shard_map/all_to_all | solution.py:561
  9.1 0.0 copy-done
  9.1 0.0 copy-done.1
  9.1 0.0 copy-done.2
  9.1 0.2 inner_1.1.rate
  9.3 0.0 copy-start.3
  9.3 5.4 %all-to-all-done.planes = f32[8,56,128]{2,1,0:T(8,128)S(1)} async-done(((f32[8,56,128]{2,1,0:T(8,128)}), f32[8,56,128]{2,1,0:T(8,128)S(1)}, u32[]{:S(2)}, u32[]{:S(2)}) %all-to-all-start) | async-done | bytes 229408 | tf_op jit(solution)/shard_map/all_to_all | solution.py:561
  14.8 1.0 %section_1.1 = (f32[5,8,8,128]{3,2,1,0:T(8,128)S(1)}, f32[5,8,8,128]{3,2,1,0:T(8,128)S(1)}, f32[14,8,128]{2,1,0:T(8,128)S(1)}, f32[8,8,128]{2,1,0:T(8,128)S(1)}) custom-call(f32[5,8,8,128]{3,2,1,0:T(8,128)S(1)} %copy-done, f32[5,8,8,128]{3,2,1,0:T(8,128)S(1)} %inner_1.1.rate, f32[8,56,128]{2,1,0:T(8,128)S(1)} %all-to-all-done.planes, f32[19,8,128]{2,1,0:T(8,128)S(1)} %copy-done.1), custom_call_target="tpu_custom_call" | custom-call | tf_op jit(solution)/shard_map/section_1/pallas_call | solution.py:571
  15.8 4.3 %collective-permute-start = (f32[14,8,128]{2,1,0:T(8,128)S(1)}, f32[14,8,128]{2,1,0:T(8,128)S(1)}, u32[]{:S(2)}, u32[]{:S(2)}) collective-permute-start(f32[14,8,128]{2,1,0:T(8,128)S(1)} %get-tuple-element.27), channel_id=1, source_target_pairs={{0,8},{8,16},{16,24},{24,32},{32,40},{40,48},{48,56},{56,64},{64,7... | collective-permute-start | bytes 172040 | tf_op jit(solution)/shard_map/ppermute | solution.py:504
  20.1 0.0 copy-done.3
  20.1 12.1 %collective-permute-start.1 = (f32[5,8,128]{2,1,0:T(8,128)S(1)}, f32[5,8,128]{2,1,0:T(8,128)S(1)}, u32[]{:S(2)}, u32[]{:S(2)}) collective-permute-start(f32[5,8,128]{2,1,0:T(8,128)S(1)} %copy-done.3), channel_id=1, source_target_pairs={{8,0},{16,8},{24,16},{32,24},{40,32},{48,40},{56,48},{64,56},{72,6... | collective-permute-start | bytes 61448 | tf_op jit(solution)/shard_map/ppermute | solution.py:504
  32.2 1.5 %collective-permute-done.1.ahead = f32[5,8,128]{2,1,0:T(8,128)S(1)} collective-permute-done((f32[5,8,128]{2,1,0:T(8,128)S(1)}, f32[5,8,128]{2,1,0:T(8,128)S(1)}, u32[]{:S(2)}, u32[]{:S(2)}) %collective-permute-start.1) | collective-permute-done | bytes 20512 | tf_op jit(solution)/shard_map/ppermute | solution.py:504
  33.7 0.0 collective-permute-done.behind
  33.7 1.5 %sample_2.1 = (f32[5,8,8,128]{3,2,1,0:T(8,128)S(1)}, f32[5,8,8,128]{3,2,1,0:T(8,128)S(1)}, f32[8,48,128]{2,1,0:T(8,128)}, f32[5,8,128]{2,1,0:T(8,128)S(1)}, bf16...) custom-call(f32[5,8,8,128]{3,2,1,0:T(8,128)S(1)} %get-tuple-element.25.stat, ...), custom_call_target="tpu_custom_call" | custom-call | tf_op jit(solution)/shard_map/sample_2/pallas_call | solution.py:581
  35.2 4.8 %all-to-all-start.1 = ((f32[8,48,128]{2,1,0:T(8,128)}), f32[8,48,128]{2,1,0:T(8,128)S(1)}, u32[]{:S(2)}, u32[]{:S(2)}) async-start(f32[8,48,128]{2,1,0:T(8,128)} %get-tuple-element.39), calls=%async_computation.1 | async-start | bytes 393216 | tf_op jit(solution)/shard_map/all_to_all | solution.py:599
  40.0 7.5 %collective-permute-start.2 = (f32[5,8,128]{2,1,0:T(8,128)S(1)}, f32[5,8,128]{2,1,0:T(8,128)S(1)}, u32[]{:S(2)}, u32[]{:S(2)}) collective-permute-start(f32[5,8,128]{2,1,0:T(8,128)S(1)} %get-tuple-element.38), channel_id=1, source_target_pairs={{8,0},{16,8},{24,16},{32,24},{40,32},{48,40},{56,48},{64,56},{72,6... | collective-permute-start | bytes 61448 | tf_op jit(solution)/shard_map/ppermute | solution.py:504
  47.5 0.7 %inner_2.1 = (f32[5,8,8,128]{3,2,1,0:T(8,128)S(1)}, f32[5,8,8,128]{3,2,1,0:T(8,128)S(1)}) custom-call(f32[5,8,8,128]{3,2,1,0:T(8,128)S(1)} %get-tuple-element.30.state, f32[5,8,8,128]{3,2,1,0:T(8,128)S(1)} %get-tuple-element.31.reg_in, f32[5,8,8,128]{3,2,1,0:T(8,128)S(1)} %copy-done, f32[14,8,128]{2,1,0:T(8,128)S(1)} %collective-permute-done.behind, ...), custom_call_target="tpu_custom_call" | custom-call | tf_op jit(solution)/shard_map/inner_2/pallas_call | solution.py:601
  48.2 0.8 %collective-permute-done.2.ahead = f32[5,8,128]{2,1,0:T(8,128)S(1)} collective-permute-done((f32[5,8,128]{2,1,0:T(8,128)S(1)}, f32[5,8,128]{2,1,0:T(8,128)S(1)}, u32[]{:S(2)}, u32[]{:S(2)}) %collective-permute-start.2) | collective-permute-done | bytes 20512 | tf_op jit(solution)/shard_map/ppermute | solution.py:504
  49.0 0.0 all-to-all-done.1.returned
  49.0 0.8 %last.1 = (f32[5,8,8,128]{3,2,1,0:T(8,128)}, f32[5,8,8,128]{3,2,1,0:T(8,128)}, f32[3,8,128]{2,1,0:T(8,128)}, f32[3,8,128]{2,1,0:T(8,128)}) custom-call(f32[5,8,8,128]{3,2,1,0:T(8,128)S(1)} %get-tuple-element.36.state, f32[5,8,8,128]{3,2,1,0:T(8,128)S(1)} %get-tuple-element.37.reg_in, f32[5,8,128]{2,1,0:T(8,128)S(1)} %collective-permute-done.2.ahead, ...), custom_call_target="tpu_custom_call" | custom-call | tf_op jit(solution)/shard_map/last/pallas_call | solution.py:610
Async XLA Ops:
  4.1 5.0 %copy-start = (f32[5,8,8,128]{3,2,1,0:T(8,128)S(1)}, f32[5,8,8,128]{3,2,1,0:T(8,128)}, u32[]{:S(2)}) copy-start(f32[5,8,8,128]{3,2,1,0:T(8,128)} %start.1) | copy-start | bytes 491524
  4.1 5.0 %copy-start.1 = (f32[19,8,128]{2,1,0:T(8,128)S(1)}, f32[19,8,128]{2,1,0:T(8,128)}, u32[]{:S(2)}) copy-start(f32[19,8,128]{2,1,0:T(8,128)} %constant.4.clone.cols_ref) | copy-start | bytes 233476
  4.1 5.0 %copy-start.2 = (bf16[384,128]{1,0:T(8,128)(2,1)S(1)}, bf16[384,128]{1,0:T(8,128)(2,1)}, u32[]{:S(2)}) copy-start(bf16[384,128]{1,0:T(8,128)(2,1)} %constant.5.clone.mz) | copy-start | bytes 294916
  4.1 10.7 %all-to-all-start = ((f32[8,56,128]{2,1,0:T(8,128)}), f32[8,56,128]{2,1,0:T(8,128)S(1)}, u32[]{:S(2)}, u32[]{:S(2)}) async-start(f32[8,56,128]{2,1,0:T(8,128)} %get-tuple-element.24), calls=%async_computation | async-start | bytes 458752 | tf_op jit(solution)/shard_map/all_to_all | solution.py:561
  9.3 10.8 %copy-start.3 = (f32[5,8,128]{2,1,0:T(8,128)S(1)}, f32[5,8,128]{2,1,0:T(8,128)}, u32[]{:S(2)}) copy-start(f32[5,8,128]{2,1,0:T(8,128)} %get-tuple-element.28) | copy-start | bytes 61444
  15.8 17.9 %collective-permute-start = (f32[14,8,128]{2,1,0:T(8,128)S(1)}, f32[14,8,128]{2,1,0:T(8,128)S(1)}, u32[]{:S(2)}, u32[]{:S(2)}) collective-permute-start(f32[14,8,128]{2,1,0:T(8,128)S(1)} %get-tuple-element.27), channel_id=1, source_target_pairs={{0,8},{8,16},{16,24},{24,32},{32,40},{40,48},{48,56},{56,64},{64,7... | collective-permute-start | bytes 172040 | tf_op jit(solution)/shard_map/ppermute | solution.py:504
  20.1 13.6 %collective-permute-start.1 = (f32[5,8,128]{2,1,0:T(8,128)S(1)}, f32[5,8,128]{2,1,0:T(8,128)S(1)}, u32[]{:S(2)}, u32[]{:S(2)}) collective-permute-start(f32[5,8,128]{2,1,0:T(8,128)S(1)} %copy-done.3), channel_id=1, source_target_pairs={{8,0},{16,8},{24,16},{32,24},{40,32},{48,40},{56,48},{64,56},{72,6... | collective-permute-start | bytes 61448 | tf_op jit(solution)/shard_map/ppermute | solution.py:504
  35.2 13.7 %all-to-all-start.1 = ((f32[8,48,128]{2,1,0:T(8,128)}), f32[8,48,128]{2,1,0:T(8,128)S(1)}, u32[]{:S(2)}, u32[]{:S(2)}) async-start(f32[8,48,128]{2,1,0:T(8,128)} %get-tuple-element.39), calls=%async_computation.1 | async-start | bytes 393216 | tf_op jit(solution)/shard_map/all_to_all | solution.py:599
  40.0 9.0 %collective-permute-start.2 = (f32[5,8,128]{2,1,0:T(8,128)S(1)}, f32[5,8,128]{2,1,0:T(8,128)S(1)}, u32[]{:S(2)}, u32[]{:S(2)}) collective-permute-start(f32[5,8,128]{2,1,0:T(8,128)S(1)} %get-tuple-element.38), channel_id=1, source_target_pairs={{8,0},{16,8},{24,16},{32,24},{40,32},{48,40},{56,48},{64,56},{72,6... | collective-permute-start | bytes 61448 | tf_op jit(solution)/shard_map/ppermute | solution.py:504
